TPU v7x, 512 devices: a whole 4x8x8 slice. The times are simulated.
512 devices in a mesh: head: 8 (over x, core), ctx: 64 (over z, y).
Axes of the slice: x: 4, y: 8, z: 8, core: 2. Of those that a mesh axis runs over, the one named last changes fastest.
Arguments:
- queries: bfloat16 [8192, 6144], P('ctx', 'head'), may hold values from -6 to 6
- key_rows: bfloat16 [8192, 1024], P('ctx', 'head'), may hold values from -6 to 6
- value_rows: bfloat16 [8192, 1024], P('ctx', 'head'), may hold values from -6 to 6
- out_grad: bfloat16 [8192, 6144], P('ctx', 'head'), may hold values from -24 to 24
- gate_logit: float32 [8192], P('ctx'), may hold values from -6 to 6
- tile_plan: int32 [64, 4, 64], replicated, may hold values from -1 to 15, as said below
- mask_kind: int32 [64, 4, 64], P('ctx'), may hold values from 0 to 1
Outputs:
- query_grad: bfloat16 [8192, 6144], P('ctx', 'head')
- key_grad: bfloat16 [8192, 1024], P('ctx', 'head')
- value_grad: bfloat16 [8192, 1024], P('ctx', 'head')
- gate_grad: float32 [8192], P('ctx')
Inputs may be any that keep to these rules, and one draw needn't show every extreme that they name: tile_plan[b, s, p] is a key tile of block p (of 8 rows) that block b reads in section s, or -1; it is -1 when p == b; the tiles that b reads from one p differ from section to section; in every section each block reads from between 16 and 32 blocks, and some block reads from exactly 32.
All inputs are finite; a program needn't handle non-finite values.
Results may differ from a plain program's by a relative error of at most 0.033.
Values may be sent and summed in bfloat16 or wider, within the bound.
No kernel may reach another device: no remote copies, remote signals or barrier semaphores. Data moves between devices by JAX's collectives and lax.ppermute only.
A program may use at most 64 MiB of HBM per device.

v0:
```python
import math

import jax
import jax.numpy as jnp
from jax import lax
from jax.sharding import PartitionSpec as P

HD = 128
TILE = 8
SECTIONS = 4


big_negative = -1e30


def over_pieces(x, axis):
    return lax.all_gather(x, axis).sum(0)


def body(queries, key_rows, value_rows, out_grad, gate_logit, tile_plan, mask_kind):
    row_count = queries.shape[0]
    kv_count = key_rows.shape[1] // HD
    head_count = queries.shape[1] // HD
    group_size = head_count // kv_count
    kv_width = kv_count * HD
    tile_count = row_count // TILE
    peer_count = lax.axis_size("ctx")
    device = lax.axis_index("ctx")
    factor = 1.0 / math.sqrt(HD)
    row_index = jnp.arange(row_count, dtype=jnp.int32)
    late_rows = row_index >= row_count // 2
    tile_index = jnp.arange(tile_count, dtype=jnp.int32)
    plan_read = lax.dynamic_index_in_dim(tile_plan, device, 0, keepdims=False)
    plan_given = lax.dynamic_index_in_dim(tile_plan, device, 2, keepdims=False)
    slot_order = jnp.broadcast_to(
        jnp.arange(peer_count, dtype=jnp.int32)[None, :], (SECTIONS, peer_count)
    )
    slot_tiles = jnp.take_along_axis(plan_read, slot_order, axis=1)
    slot_kinds = jnp.take_along_axis(mask_kind[0], slot_order, axis=1)
    slot_seen = (slot_tiles >= 0)[None] & ((slot_kinds == 0)[None] | late_rows[:, None, None])
    joined = jnp.concatenate([key_rows, value_rows], axis=1).reshape(tile_count, TILE, 2 * kv_width)
    outgoing = jnp.where(
        (plan_given >= 0)[:, :, None, None],
        joined[jnp.maximum(plan_given, 0)],
        jnp.zeros((), jnp.bfloat16),
    )
    arrived = lax.all_to_all(outgoing, "ctx", split_axis=0, concat_axis=0, tiled=True)
    fetched = [arrived[:, section_index] for section_index in range(SECTIONS)]
    key_sets = [
        (
            key_rows.reshape(row_count, kv_count, HD),
            value_rows.reshape(row_count, kv_count, HD),
            row_index[:, None] >= row_index[None, :],
        )
    ]
    for section_index in range(SECTIONS):
        picked = fetched[section_index]
        picked = picked.reshape(peer_count * TILE, 2 * kv_width)
        visible = jnp.broadcast_to(
            slot_seen[:, section_index, :, None], (row_count, peer_count, TILE)
        ).reshape(row_count, peer_count * TILE)
        key_sets.append(
            (
                picked[:, :kv_width].reshape(-1, kv_count, HD),
                picked[:, kv_width:].reshape(-1, kv_count, HD),
                visible,
            )
        )
    query_heads = queries.reshape(row_count, kv_count, group_size, HD)
    grad_heads = out_grad.reshape(row_count, kv_count, group_size, HD)
    gate = jax.nn.sigmoid(gate_logit)
    d_attended = (gate[:, None, None, None] * grad_heads.astype(jnp.float32)).astype(jnp.bfloat16)
    running_top = jnp.full((kv_count, group_size, row_count), big_negative, jnp.float32)
    running_total = jnp.zeros((kv_count, group_size, row_count), jnp.float32)
    kept_scores = []
    for key_set, value_set, visible in key_sets:
        scores = (
            jnp.einsum("rcgd,kcd->cgrk", query_heads, key_set, preferred_element_type=jnp.float32)
            * factor
        )
        scores = jnp.where(visible[None, None], scores, big_negative)
        kept_scores.append(scores)
        new_top = jnp.maximum(running_top, jnp.max(scores, axis=-1))
        running_total = running_total * jnp.exp(running_top - new_top) + jnp.sum(
            jnp.exp(scores - new_top[..., None]), axis=-1
        )
        running_top = new_top
    log_total = running_top + jnp.log(running_total)
    attended_sum = jnp.zeros((row_count, kv_count, group_size, HD), jnp.float32)
    value_parts = []
    kept_probs = []
    for set_index in range(len(key_sets)):
        key_set, value_set, visible = key_sets[set_index]
        probs = jnp.exp(kept_scores[set_index] - log_total[..., None])
        kept_probs.append(probs)
        probs_low = probs.astype(jnp.bfloat16)
        attended_sum = attended_sum + jnp.einsum(
            "cgrk,kcd->rcgd", probs_low, value_set, preferred_element_type=jnp.float32
        )
        value_parts.append(
            jnp.einsum("cgrk,rcgd->kcd", probs_low, d_attended, preferred_element_type=jnp.float32)
        )
    attended = attended_sum.astype(jnp.bfloat16).astype(jnp.float32)
    gate_part = jnp.sum(grad_heads.astype(jnp.float32) * attended, axis=(1, 2, 3))
    gate_sum = over_pieces(gate_part, "head")
    gate_grad = gate * (1.0 - gate) * gate_sum
    delta = jnp.transpose(jnp.sum(d_attended.astype(jnp.float32) * attended, axis=-1), (1, 2, 0))
    query_sum = jnp.zeros((row_count, kv_count, group_size, HD), jnp.float32)
    grad_parts = []
    for set_index in range(len(key_sets)):
        key_set, value_set, visible = key_sets[set_index]
        probs = kept_probs[set_index]
        d_probs = jnp.einsum(
            "rcgd,kcd->cgrk", d_attended, value_set, preferred_element_type=jnp.float32
        )
        d_scores = (probs * (d_probs - delta[..., None])).astype(jnp.bfloat16)
        query_sum = query_sum + jnp.einsum(
            "cgrk,kcd->rcgd", d_scores, key_set, preferred_element_type=jnp.float32
        )
        key_part = (
            jnp.einsum("cgrk,rcgd->kcd", d_scores, query_heads, preferred_element_type=jnp.float32)
            * factor
        )
        both_parts = jnp.concatenate(
            [key_part.reshape(-1, kv_width), value_parts[set_index].reshape(-1, kv_width)], axis=1
        )
        grad_parts.append(both_parts)
    returns = []
    for section_index in range(SECTIONS):
        slot_part = grad_parts[section_index + 1].reshape(peer_count, TILE, 2 * kv_width)
        returns.append(slot_part)
    returned_all = lax.all_to_all(
        jnp.stack(returns, axis=1).astype(jnp.bfloat16),
        "ctx",
        split_axis=0,
        concat_axis=0,
        tiled=True,
    ).astype(jnp.float32)
    owners = (plan_given[:, :, None] == tile_index[None, None, :]).astype(jnp.float32)
    owner_sum = jnp.einsum("nst,nsrc->trc", owners, returned_all, precision=lax.Precision.HIGHEST)
    local_sum = grad_parts[0] + owner_sum.reshape(row_count, 2 * kv_width)
    query_grad = (query_sum * factor).reshape(row_count, head_count * HD).astype(jnp.bfloat16)
    key_grad = local_sum[:, :kv_width].astype(jnp.bfloat16)
    value_grad = local_sum[:, kv_width:].astype(jnp.bfloat16)
    return (query_grad, key_grad, value_grad, gate_grad)


def solution(mesh):
    placed = (
        P("ctx", "head"),
        P("ctx", "head"),
        P("ctx", "head"),
        P("ctx", "head"),
        P("ctx"),
        P(),
        P("ctx", None, None),
    )
    return jax.shard_map(
        body,
        mesh=mesh,
        in_specs=placed,
        out_specs=(P("ctx", "head"), P("ctx", "head"), P("ctx", "head"), P("ctx")),
        check_vma=False,
    )
```

profile of v0, /device:TPU:6, one launch (start us, length us, event | category | flops | bytes accessed | tf_op | source)
XLA Modules:
  0.0 114.7 jit_solution(6827345424757636721)
XLA Ops:
  0.6 2.2 %maximum_reduce_fusion = (s32[64,4]{1,0:T(8,128)S(1)}, s32[64,4,1]{2,1,0:T(4,128)S(1)}) fusion(s32[64,4,64]{2,1,0:T(4,128)} %param.14, s32[]{:T(128)S(6)} %select_n.35), kind=kLoop, calls=%fused_computation.126 | loop fusion | flops 256 | bytes 3076 | tf_op jit(solution)/shard_map/max | solution.py:44
  2.8 0.1 reshape.564
  3.0 0.1 copy.132
  3.2 0.8 maximum_bitcast_fusion
  3.9 0.8 gather_fusion
  4.7 1.3 %broadcast_select_fusion = bf16[64,4,8,256]{3,2,1,0:T(8,128)(2,1)} fusion(bf16[64,4,8,256]{3,2,1,0:T(8,128)(2,1)S(1)} %bitcast.441, pred[64,4]{1,0:T(8,128)(4,1)S(1)} %copy.132), kind=kLoop, calls=%fused_computation.93 | loop fusion | flops 524288 | bytes 2097408 | tf_op jit(solution)/shard_map/jit(_where)/select_n | solution.py:42
  6.0 16.8 %all-to-all-start = ((bf16[64,4,8,256]{3,2,1,0:T(8,128)(2,1)}), bf16[64,4,8,256]{3,2,1,0:T(8,128)(2,1)S(1)}, u32[]{:S(2)}, u32[]{:S(2)}) async-start(bf16[64,4,8,256]{3,2,1,0:T(8,128)(2,1)} %broadcast_select_fusion), calls=%async_computation | async-start | bytes 2097152 | tf_op jit(solution)/shard_map/all_to_all | solution.py:47
  22.7 0.7 dynamic-slice_bitcast_fusion
  23.5 2.4 %gather_fusion.1 = s32[256]{0:T(256)S(1)} fusion(s32[4,64]{1,0:T(4,128)S(1)} %dynamic-slice_bitcast_fusion, s32[256]{0:T(256)S(1)} %reshape.586), kind=kCustom, calls=%fused_computation.clone | custom fusion | bytes 4096 | tf_op jit(solution)/shard_map/jit(take_along_axis)/gather | solution.py:38
  26.0 2.4 %gather_fusion.2 = s32[256]{0:T(256)S(1)} fusion(s32[4,64]{1,0:T(4,128)S(1)} %bitcast.425, s32[256]{0:T(256)S(1)} %reshape.586), kind=kCustom, calls=%fused_computation.1.clone | custom fusion | bytes 4096 | tf_op jit(solution)/shard_map/jit(take_along_axis)/gather | solution.py:39
  28.6 0.2 copy.137
  28.9 0.2 copy.129
  29.0 0.1 or_and_fusion
  29.5 0.2 fusion.106
  29.7 22.6 %all-to-all-done = bf16[64,4,8,256]{3,2,1,0:T(8,128)(2,1)S(1)} async-done(((bf16[64,4,8,256]{3,2,1,0:T(8,128)(2,1)}), bf16[64,4,8,256]{3,2,1,0:T(8,128)(2,1)S(1)}, u32[]{:S(2)}, u32[]{:S(2)}) %all-to-all-start) | async-done | bytes 1048608 | tf_op jit(solution)/shard_map/all_to_all | solution.py:47
  52.4 0.4 fusion.105
  52.8 0.4 fusion.102
  53.2 0.4 fusion.103
  53.6 0.4 fusion.104
  54.0 0.2 exponential_reduce_fusion
  54.3 0.2 exponential_reduce_fusion.1
  54.5 0.2 exponential_reduce_fusion.2
  54.7 0.2 exponential_reduce_fusion.3
  55.0 1.1 fusion.48
  56.1 1.1 fusion.49
  57.1 0.4 fusion.50
  57.5 1.1 fusion.51
  58.6 0.4 fusion.67
  59.0 0.4 fusion.70
  59.4 0.4 fusion.73
  59.9 0.4 fusion.64
  60.3 0.3 copy-done.12
  60.6 0.9 multiply_reduce_fusion
  61.5 0.4 fusion.13
  61.9 0.4 fusion.14
  62.4 0.4 fusion.15
  62.8 1.4 %fusion.12 = bf16[6,128,512]{1,2,0:T(8,128)(2,1)} fusion(bf16[128,6,128]{0,2,1:T(8,128)(2,1)S(1)} %bitcast.439, f32[1,6,128,512]{2,3,1,0:T(8,128)S(1)} %get-tuple-element.43, f32[6,128]{1,0:T(8,128)S(1)} %bitcast.453, f32[6,128]{1,0:T(8,128)S(1)} %log_add_fusion, bf16[512,256]{1,0:T(8,128)(2,1)S(1)} %get-tuple-element.25), kind=kOutput, calls=%fused_computation.31 | convolution fusion | flops 102236160 | bytes 2695168 | tf_op jit(solution)/shard_map/rcgd,kcd->cgrk/dot_general | solution.py:113
  64.2 1.6 %copy.177 = bf16[512,1,128]{2,0,1:T(8,128)(2,1)} copy(bf16[512,1,128]{0,2,1:T(8,128)(2,1)} %fusion.48) | data formatting | bytes 262144 | tf_op jit(solution)/shard_map/cgrk,rcgd->kcd/transpose | solution.py:101
  65.8 1.7 %copy.174 = bf16[512,1,128]{2,0,1:T(8,128)(2,1)} copy(bf16[512,1,128]{0,2,1:T(8,128)(2,1)} %fusion.49) | data formatting | bytes 262144 | tf_op jit(solution)/shard_map/cgrk,rcgd->kcd/transpose | solution.py:101
  67.5 1.7 %copy.168 = bf16[512,1,128]{2,0,1:T(8,128)(2,1)} copy(bf16[512,1,128]{0,2,1:T(8,128)(2,1)} %fusion.51) | data formatting | bytes 262144 | tf_op jit(solution)/shard_map/cgrk,rcgd->kcd/transpose | solution.py:101
  69.2 0.8 copy.171
  69.9 1.5 %fusion.55 = bf16[64,1,8,128]{3,2,0,1:T(8,128)(2,1)S(1)} fusion(bf16[6,128,512]{1,2,0:T(8,128)(2,1)} %fusion.12, bf16[128,6,128]{0,2,1:T(8,128)(2,1)S(1)} %bitcast.431), kind=kOutput, calls=%fused_computation.87 | convolution fusion | flops 100794368 | bytes 1114112 | tf_op jit(solution)/shard_map/cgrk,rcgd->kcd/dot_general | solution.py:121
  71.5 0.4 fusion.52
  71.8 0.4 fusion.53
  72.2 0.4 fusion.54
  72.6 0.1 maximum_maximum_fusion
  72.7 2.4 %copy.178 = bf16[64,4,8,256]{3,1,2,0:T(4,128)(2,1)} copy(bf16[64,4,8,256]{3,2,0,1:T(8,128)(2,1)S(1)} %maximum_maximum_fusion) | data formatting | bytes 2097152 | tf_op jit(solution)/shard_map/stack | solution.py:133
  75.1 6.7 %all-to-all-start.1 = ((bf16[64,4,8,256]{3,1,2,0:T(4,128)(2,1)}), bf16[64,4,8,256]{3,1,2,0:T(4,128)(2,1)}, u32[]{:S(2)}, u32[]{:S(2)}) async-start(bf16[64,4,8,256]{3,1,2,0:T(4,128)(2,1)} %copy.178), calls=%async_computation.1 | async-start | bytes 2097152 | tf_op jit(solution)/shard_map/all_to_all | solution.py:132
  81.9 1.0 fusion.36
  82.9 1.5 %fusion.77 = f32[128,6,128]{2,0,1:T(8,128)S(1)} fusion(bf16[6,128,512]{1,2,0:T(8,128)(2,1)} %fusion.12, bf16[512,256]{1,0:T(8,128)(2,1)} %copy-done.7), kind=kOutput, calls=%fused_computation.132 | convolution fusion | flops 100663296 | bytes 1310720 | tf_op jit(solution)/shard_map/cgrk,kcd->rcgd/dot_general | solution.py:117
  84.5 0.3 fusion.80
  84.8 0.3 fusion.79
  85.1 0.3 copy-done.2
  85.4 0.3 fusion.78
  85.7 0.3 fusion.28
  86.0 0.8 copy.182
  86.9 7.4 %all-gather.1 = f32[8,1,128]{2,1,0:T(1,128)S(1)} all-gather(f32[1,1,128]{2,1,0:T(1,128)S(1)} %bitcast.456), channel_id=2, replica_groups=mesh['head'=8,'ctx'=64] {'head'}, dimensions={0}, use_global_device_ids=true | all-gather | bytes 4608 | tf_op jit(solution)/shard_map/all_gather | solution.py:17
  94.3 0.2 convolution_bitcast_fusion.12
  94.6 0.5 fusion.97
  95.1 0.2 fusion.56
  95.3 15.3 %all-to-all-done.1 = bf16[64,4,8,256]{3,1,2,0:T(4,128)(2,1)} async-done(((bf16[64,4,8,256]{3,1,2,0:T(4,128)(2,1)}), bf16[64,4,8,256]{3,1,2,0:T(4,128)(2,1)}, u32[]{:S(2)}, u32[]{:S(2)}) %all-to-all-start.1) | async-done | bytes 1048608 | tf_op jit(solution)/shard_map/all_to_all | solution.py:132
  110.6 2.4 %convolution_bitcast_fusion.11 = f32[16,8,256]{2,0,1:T(8,128)S(1)} fusion(bf16[64,4,8,256]{3,1,2,0:T(4,128)(2,1)} %all-to-all-done.1, s32[64,4]{0,1:T(4,128)S(1)} %bitcast.455), kind=kOutput, calls=%fused_computation.83 | convolution fusion | flops 16781312 | bytes 1180672 | tf_op jit(solution)/shard_map/nst,nsrc->trc/dot_general | solution.py:140
  113.3 0.7 copy.184
  114.0 0.7 copy.183
  (66 shorter events, 1.2 us)
Async XLA Ops:
  0.6 25.3 %copy-start = (s32[1,4,64]{2,1,0:T(4,128)S(1)}, s32[1,4,64]{2,1,0:T(4,128)}, u32[]{:S(2)}) copy-start(s32[1,4,64]{2,1,0:T(4,128)} %param.15) | copy-start | bytes 3076
  6.0 46.4 %all-to-all-start = ((bf16[64,4,8,256]{3,2,1,0:T(8,128)(2,1)}), bf16[64,4,8,256]{3,2,1,0:T(8,128)(2,1)S(1)}, u32[]{:S(2)}, u32[]{:S(2)}) async-start(bf16[64,4,8,256]{3,2,1,0:T(8,128)(2,1)} %broadcast_select_fusion), calls=%async_computation | async-start | bytes 2097152 | tf_op jit(solution)/shard_map/all_to_all | solution.py:47
  26.0 2.7 %copy-start.15 = (bf16[128,768]{1,0:T(8,128)(2,1)S(1)}, bf16[128,768]{1,0:T(8,128)(2,1)}, u32[]{:S(2)}) copy-start(bf16[128,768]{1,0:T(8,128)(2,1)} %param.12) | copy-start | bytes 589828
  26.0 2.8 %copy-start.16 = (bf16[128,768]{1,0:T(8,128)(2,1)S(1)}, bf16[128,768]{1,0:T(8,128)(2,1)}, u32[]{:S(2)}) copy-start(bf16[128,768]{1,0:T(8,128)(2,1)} %param.9) | copy-start | bytes 589828
  26.0 3.2 %copy-start.18 = (f32[128]{0:T(128)S(1)}, f32[128]{0:T(128)}, u32[]{:S(2)}) copy-start(f32[128]{0:T(128)} %param.13) | copy-start | bytes 1540
  28.5 1.0 copy-start.13
  52.4 9.1 %copy-start.1 = (bf16[512,256]{1,0:T(8,128)(2,1)}, bf16[512,256]{1,0:T(8,128)(2,1)S(1)}, u32[]{:S(2)}) copy-start(bf16[512,256]{1,0:T(8,128)(2,1)S(1)} %get-tuple-element.28) | copy-start | bytes 786436
  52.4 9.6 %copy-start.3 = (bf16[512,256]{1,0:T(8,128)(2,1)}, bf16[512,256]{1,0:T(8,128)(2,1)S(1)}, u32[]{:S(2)}) copy-start(bf16[512,256]{1,0:T(8,128)(2,1)S(1)} %get-tuple-element.27) | copy-start | bytes 786436
  52.4 10.0 %copy-start.5 = (bf16[512,256]{1,0:T(8,128)(2,1)}, bf16[512,256]{1,0:T(8,128)(2,1)S(1)}, u32[]{:S(2)}) copy-start(bf16[512,256]{1,0:T(8,128)(2,1)S(1)} %get-tuple-element.26) | copy-start | bytes 786436
  52.4 10.4 %copy-start.7 = (bf16[512,256]{1,0:T(8,128)(2,1)}, bf16[512,256]{1,0:T(8,128)(2,1)S(1)}, u32[]{:S(2)}) copy-start(bf16[512,256]{1,0:T(8,128)(2,1)S(1)} %get-tuple-element.25) | copy-start | bytes 786436
  59.9 0.8 copy-start.12
  71.4 1.2 %copy-start.8 = (bf16[512,1,128]{2,0,1:T(8,128)(2,1)S(1)}, bf16[512,1,128]{2,0,1:T(8,128)(2,1)}, u32[]{:S(2)}) copy-start(bf16[512,1,128]{2,0,1:T(8,128)(2,1)} %copy.177) | copy-start | bytes 393220
  71.4 1.2 %copy-start.9 = (bf16[512,1,128]{2,0,1:T(8,128)(2,1)S(1)}, bf16[512,1,128]{2,0,1:T(8,128)(2,1)}, u32[]{:S(2)}) copy-start(bf16[512,1,128]{2,0,1:T(8,128)(2,1)} %copy.174) | copy-start | bytes 393220
  71.4 1.2 %copy-start.10 = (bf16[512,1,128]{2,0,1:T(8,128)(2,1)S(1)}, bf16[512,1,128]{2,0,1:T(8,128)(2,1)}, u32[]{:S(2)}) copy-start(bf16[512,1,128]{2,0,1:T(8,128)(2,1)} %copy.168) | copy-start | bytes 393220
  71.5 1.2 %copy-start.11 = (bf16[512,1,128]{2,0,1:T(8,128)(2,1)S(1)}, bf16[512,1,128]{2,0,1:T(8,128)(2,1)}, u32[]{:S(2)}) copy-start(bf16[512,1,128]{2,0,1:T(8,128)(2,1)} %copy.171) | copy-start | bytes 393220
  75.1 35.5 %all-to-all-start.1 = ((bf16[64,4,8,256]{3,1,2,0:T(4,128)(2,1)}), bf16[64,4,8,256]{3,1,2,0:T(4,128)(2,1)}, u32[]{:S(2)}, u32[]{:S(2)}) async-start(bf16[64,4,8,256]{3,1,2,0:T(4,128)(2,1)} %copy.178), calls=%async_computation.1 | async-start | bytes 2097152 | tf_op jit(solution)/shard_map/all_to_all | solution.py:132
  81.9 2.6 %copy-start.6 = (bf16[512,256]{1,0:T(8,128)(2,1)S(1)}, bf16[512,256]{1,0:T(8,128)(2,1)}, u32[]{:S(2)}) copy-start(bf16[512,256]{1,0:T(8,128)(2,1)} %copy-done.5) | copy-start | bytes 786436
  81.9 2.9 %copy-start.4 = (bf16[512,256]{1,0:T(8,128)(2,1)S(1)}, bf16[512,256]{1,0:T(8,128)(2,1)}, u32[]{:S(2)}) copy-start(bf16[512,256]{1,0:T(8,128)(2,1)} %copy-done.3) | copy-start | bytes 786436
  84.5 1.0 copy-start.2
  84.8 0.9 copy-start.14
  85.4 1.5 %copy-start.17 = (f32[128]{0:T(128)S(1)}, f32[128]{0:T(128)}, u32[]{:S(2)}) copy-start(f32[128]{0:T(128)} %get-tuple-element.17) | copy-start | bytes 1540
  85.7 8.8 %copy-start.19 = (f32[128]{0:T(128)S(1)}, f32[128]{0:T(128)}, u32[]{:S(2)}) copy-start(f32[128]{0:T(128)} %param.13) | copy-start | bytes 1540
where the time goes:
time: 115 us
  waiting for transfers between devices  37.9 us (33%)
  starting transfers between devices  23.5 us (20%)
  matrix products  19.6 us (17%)
  local copies, waits for them, and re-layouts  18.7 us (16%)
  blocking collectives  7.42 us (6%)
  other arithmetic  6.2 us (5%)
  between operations  1.31 us (1%)
    all_to_all x1, waiting for transfers between devices, body(): lax.all_to_all(outgoing, 'ctx', split_axis=0, concat_axis=0, tiled=True)  22.6 us
    all_to_all x1, starting transfers between devices, body(): lax.all_to_all(outgoing, 'ctx', split_axis=0, concat_axis=0, tiled=True)  16.8 us
    all_to_all x1, waiting for transfers between devices, body(): lax.all_to_all(jnp.stack(returns, axis=1).astype(jnp.bfloat16), 'ctx', sp...  15.3 us
    all_gather x1, blocking collectives, over_pieces(): return lax.all_gather(x, axis).sum(0)  7.42 us
    all_to_all x1, starting transfers between devices, body(): lax.all_to_all(jnp.stack(returns, axis=1).astype(jnp.bfloat16), 'ctx', sp...  6.75 us
    transpose x4, local copies, waits for them, and re-layouts, body(): jnp.einsum('cgrk,rcgd->kcd', probs_low, d_attended, preferred_element_typ...  5.73 us
    dot_general x5, matrix products, body(): jnp.einsum('cgrk,rcgd->kcd', probs_low, d_attended, preferred_element_typ...  3.84 us
    dot_general x5, matrix products, body(): jnp.einsum('rcgd,kcd->cgrk', d_attended, value_set, preferred_element_typ...  3.63 us
  transfers between devices with their start and end apart: 2, of which 2 were waited for; matrix products, arithmetic and copies ran while one was open for 11% of the time, Pallas kernels for 0%

commit v1 on v0

v1 whole, which is shorter than its diff:
```python
import math

import jax
import jax.numpy as jnp
from jax import lax
from jax.experimental import pallas as pl
from jax.experimental.pallas import tpu as pltpu
from jax.sharding import PartitionSpec as P

HD = 128
TILE = 8
SECTIONS = 4
ROWS = 128
PEERS = 64
GROUP = 6
SLOTS = PEERS * SECTIONS
KEYS = SLOTS * TILE
WIDE = GROUP * ROWS
CHUNK = 256
N_CHUNK = KEYS // CHUNK
FACTOR = 1.0 / math.sqrt(HD)
SCALE = FACTOR * math.log2(math.e)
HIDDEN = -1e30
INTERPRET = False
VMEM_LIMIT = 40 * 1024 * 1024

f32 = jnp.float32
bf16 = jnp.bfloat16


def dot(a, b):
    return lax.dot_general(a, b, (((1,), (0,)), ((), ())), preferred_element_type=f32)


def head(h):
    return slice(h * HD, (h + 1) * HD)


def expand(slot_values):
    wide = jnp.broadcast_to(slot_values[:, None, :], (slot_values.shape[0], TILE, HD))
    return wide.reshape(slot_values.shape[0] * TILE, HD)


def owner_matrix(plan_ref, slot_ref, device):
    for b in range(PEERS):
        slot_ref[b * SECTIONS : (b + 1) * SECTIONS, :] = plan_ref[b].astype(f32)
    pick = (lax.broadcasted_iota(jnp.int32, (PEERS, HD), 0) == device).astype(bf16)
    tiles = dot(slot_ref[...].astype(bf16), pick)
    column = lax.broadcasted_iota(jnp.int32, (KEYS, HD), 1)
    row = lax.broadcasted_iota(jnp.int32, (KEYS, HD), 0)
    wanted = jnp.where(
        (column & (TILE - 1)) == (row & (TILE - 1)), (column >> 3).astype(f32), -2.0
    )
    return jnp.where(expand(tiles) == wanted, 1.0, 0.0).astype(bf16)


def send_kernel(plan_ref, key_ref, value_ref, out_ref, slot_ref):
    matrix = owner_matrix(plan_ref, slot_ref, lax.axis_index("ctx"))
    out_ref[:, :HD] = dot(matrix, key_ref[...]).astype(bf16)
    out_ref[:, HD:] = dot(matrix, value_ref[...]).astype(bf16)


def row_gate(logit_ref):
    return jax.nn.sigmoid(logit_ref[...])


def causal_scores(key_ref, query_t):
    scores = dot(key_ref[...], query_t)
    key_at = lax.broadcasted_iota(jnp.int32, (ROWS, WIDE), 0)
    row_at = lax.broadcasted_iota(jnp.int32, (ROWS, WIDE), 1) & (ROWS - 1)
    return jnp.where(row_at >= key_at, scores, HIDDEN)


def local_kernel(
    plan_ref, kind_ref, query_ref, key_ref, value_ref, grad_ref, logit_ref,
    query_t_ref, query_s_ref, d_att_t_ref, bias_ref, start_ref, out_t_ref, slot_ref,
):
    gate = row_gate(logit_ref)
    for h in range(GROUP):
        block = query_ref[:, head(h)]
        query_s_ref[head(h), :] = block
        query_t_ref[:, head(h)] = block.astype(f32).T.astype(bf16)
        grad_t = grad_ref[:, head(h)].astype(f32).T
        d_att_t_ref[:, head(h)] = (gate * grad_t).astype(bf16)
    plan = plan_ref[lax.axis_index("ctx")]
    seen = jnp.where(plan >= 0, jnp.where(kind_ref[0] == 0, 2.0, 1.0), 0.0)
    lane = lax.broadcasted_iota(jnp.int32, (SECTIONS, PEERS), 1)
    for p in range(PEERS):
        slot_ref[p * SECTIONS : (p + 1) * SECTIONS, :] = jnp.where(lane == p, seen, 0.0)
    code = dot(slot_ref[...].astype(bf16), jnp.ones((PEERS, HD), bf16))
    need = jnp.where(lax.broadcasted_iota(jnp.int32, (SLOTS, HD), 1) >= ROWS // 2, 0.5, 1.5)
    bias_ref[...] = expand(jnp.where(code > need, 0.0, HIDDEN))
    scores = causal_scores(key_ref, query_t_ref[...])
    top = jnp.max(scores, axis=0, keepdims=True)
    weights = jnp.exp2((scores - top) * SCALE)
    start_ref[0:1, :] = top
    start_ref[1:2, :] = jnp.sum(weights, axis=0, keepdims=True)
    value_t = value_ref[...].astype(f32).T.astype(bf16)
    out_t_ref[...] = dot(value_t, weights.astype(bf16))


def main_kernel(
    kv_ref, query_t_ref, query_s_ref, d_att_t_ref, bias_ref, start_ref, out_t_ref,
    grad_ref, att_t_ref, stat_ref, score_ref, weight_ref,
):
    top = jnp.broadcast_to(start_ref[0:1, :], (TILE, WIDE))
    for c in range(N_CHUNK):
        rows = slice(c * CHUNK, (c + 1) * CHUNK)
        scores = dot(kv_ref[rows, :HD], query_t_ref[...])
        bias = bias_ref[rows, :]
        scores = scores + jnp.concatenate([bias] * GROUP, axis=1)
        score_ref[rows, :] = scores
        top = jnp.maximum(top, jnp.max(scores.reshape(CHUNK // TILE, TILE, WIDE), axis=0))
    top = jnp.max(top, axis=0, keepdims=True)
    total = jnp.zeros((TILE, WIDE), f32)
    out_t = jnp.zeros((HD, WIDE), f32)
    for c in range(N_CHUNK):
        rows = slice(c * CHUNK, (c + 1) * CHUNK)
        weights = jnp.exp2((score_ref[rows, :] - top) * SCALE)
        total = total + jnp.sum(weights.reshape(CHUNK // TILE, TILE, WIDE), axis=0)
        low = weights.astype(bf16)
        weight_ref[rows, :] = low
        out_t = out_t + dot(kv_ref[rows, HD:].T, low)
    share = jnp.exp2((start_ref[0:1, :] - top) * SCALE)
    total = jnp.sum(total, axis=0, keepdims=True) + share * start_ref[1:2, :]
    inverse = 1.0 / total
    att_t = ((out_t + share * out_t_ref[...]) * inverse).astype(bf16)
    att_t_ref[...] = att_t
    d_att_t = d_att_t_ref[...].astype(f32)
    delta = jnp.sum(d_att_t * att_t.astype(f32), axis=0, keepdims=True) * inverse
    d_low_t = (d_att_t * inverse).astype(bf16)
    d_low_s = jnp.concatenate([d_low_t[:, head(h)].T for h in range(GROUP)], axis=0)
    stat_ref[0:1, :] = top
    stat_ref[1:2, :] = inverse
    stat_ref[2:3, :] = delta
    for c in range(N_CHUNK):
        rows = slice(c * CHUNK, (c + 1) * CHUNK)
        low = weight_ref[rows, :]
        grad_ref[rows, HD:] = dot(low, d_low_s).astype(bf16)
        d_probs = dot(kv_ref[rows, HD:], d_low_t)
        d_scores = (low.astype(f32) * (d_probs - delta)).astype(bf16)
        grad_ref[rows, :HD] = (dot(d_scores, query_s_ref[...]) * FACTOR).astype(bf16)


def query_kernel(
    plan_ref, kv_ref, key_ref, value_ref, grad_ref, query_t_ref, query_s_ref, d_att_t_ref, bias_ref,
    att_t_ref, stat_ref, query_grad_ref, local_ref, gate_ref, owner_ref, slot_ref,
):
    top, inverse, delta = stat_ref[0:1, :], stat_ref[1:2, :], stat_ref[2:3, :]
    d_low_t = (d_att_t_ref[...].astype(f32) * inverse).astype(bf16)
    d_low_s = jnp.concatenate([d_low_t[:, head(h)].T for h in range(GROUP)], axis=0)

    def d_score(scores, values):
        weights = jnp.exp2((scores - top) * SCALE)
        d_scores = (weights * (dot(values, d_low_t) - delta)).astype(bf16)
        return weights.astype(bf16), d_scores

    weights, d_scores = d_score(causal_scores(key_ref, query_t_ref[...]), value_ref[...])
    local_ref[:, :HD] = dot(d_scores, query_s_ref[...]) * FACTOR
    local_ref[:, HD:] = dot(weights, d_low_s)
    total = dot(key_ref[...].T, d_scores)
    for c in range(N_CHUNK):
        rows = slice(c * CHUNK, (c + 1) * CHUNK)
        keys = kv_ref[rows, :HD]
        scores = dot(keys, query_t_ref[...]) + jnp.concatenate([bias_ref[rows, :]] * GROUP, axis=1)
        _, d_scores = d_score(scores, kv_ref[rows, HD:])
        total = total + dot(keys.T, d_scores)
    part = jnp.zeros((1, ROWS), f32)
    for h in range(GROUP):
        query_grad_ref[:, head(h)] = (total[:, head(h)] * FACTOR).T.astype(bf16)
        grad_t = grad_ref[:, head(h)].astype(f32).T
        part = part + jnp.sum(grad_t * att_t_ref[:, head(h)].astype(f32), axis=0, keepdims=True)
    gate_ref[...] = part
    matrix = owner_matrix(plan_ref, slot_ref, lax.axis_index("ctx"))
    for c in range(KEYS // HD):
        owner_ref[:, c * HD : (c + 1) * HD] = matrix[c * HD : (c + 1) * HD, :].T


def owner_kernel(owner_ref, returned_ref, local_ref, key_grad_ref, value_grad_ref):
    total = local_ref[...] + dot(owner_ref[...], returned_ref[...])
    key_grad_ref[...] = total[:, :HD].astype(bf16)
    value_grad_ref[...] = total[:, HD:].astype(bf16)


def call(kernel, outs, scratch, flops, moved, *args):
    return pl.pallas_call(
        kernel,
        out_shape=[jax.ShapeDtypeStruct(shape, kind) for shape, kind in outs],
        in_specs=[pl.BlockSpec(memory_space=pltpu.VMEM)] * len(args),
        out_specs=[pl.BlockSpec(memory_space=pltpu.VMEM)] * len(outs),
        scratch_shapes=[pltpu.VMEM(shape, kind) for shape, kind in scratch],
        compiler_params=pltpu.CompilerParams(vmem_limit_bytes=VMEM_LIMIT),
        cost_estimate=pl.CostEstimate(flops=flops, bytes_accessed=moved, transcendentals=0),
        interpret=INTERPRET,
        name=kernel.__name__,
    )(*args)


def exchange(rows):
    pieces = rows.reshape(PEERS, SECTIONS, TILE, 2 * HD)
    moved = lax.all_to_all(pieces, "ctx", split_axis=0, concat_axis=0, tiled=True)
    return moved.reshape(KEYS, 2 * HD)


def body(queries, key_rows, value_rows, out_grad, gate_logit, tile_plan, mask_kind):
    logit = gate_logit.reshape(1, ROWS)
    slot_scratch = ((SLOTS, PEERS), f32)
    (outgoing,) = call(
        send_kernel, [((KEYS, 2 * HD), bf16)], [slot_scratch], 2**27, 2**21,
        tile_plan, key_rows, value_rows,
    )
    fetched = exchange(outgoing)
    query_t, query_s, d_att_t, bias, start, out_t = call(
        local_kernel,
        [((HD, WIDE), bf16), ((WIDE, HD), bf16), ((HD, WIDE), bf16), ((KEYS, HD), f32),
         ((8, WIDE), f32), ((HD, WIDE), f32)],
        [slot_scratch], 2**27, 2**22,
        tile_plan, mask_kind, queries, key_rows, value_rows, out_grad, logit,
    )
    grads, att_t, stat = call(
        main_kernel,
        [((KEYS, 2 * HD), bf16), ((HD, WIDE), bf16), ((8, WIDE), f32)],
        [((KEYS, WIDE), f32), ((KEYS, WIDE), bf16)], 2**31, 2**22,
        fetched, query_t, query_s, d_att_t, bias, start, out_t,
    )
    returned = exchange(grads)
    query_grad, local, gate_part, owner = call(
        query_kernel,
        [((ROWS, WIDE), bf16), ((ROWS, 2 * HD), f32), ((1, ROWS), f32), ((HD, KEYS), bf16)],
        [slot_scratch], 2**31, 2**22,
        tile_plan, fetched, key_rows, value_rows, out_grad, query_t, query_s, d_att_t, bias, att_t, stat,
    )
    gate = jax.nn.sigmoid(gate_logit)
    gate_sum = lax.all_gather(gate_part[0], "head").sum(0)
    gate_grad = gate * (1.0 - gate) * gate_sum
    key_grad, value_grad = call(
        owner_kernel, [((ROWS, HD), bf16), ((ROWS, HD), bf16)], [], 2**27, 2**21,
        owner, returned, local,
    )
    return (query_grad, key_grad, value_grad, gate_grad)


def solution(mesh):
    placed = (
        P("ctx", "head"),
        P("ctx", "head"),
        P("ctx", "head"),
        P("ctx", "head"),
        P("ctx"),
        P(),
        P("ctx", None, None),
    )
    return jax.shard_map(
        body,
        mesh=mesh,
        in_specs=placed,
        out_specs=(P("ctx", "head"), P("ctx", "head"), P("ctx", "head"), P("ctx")),
        check_vma=False,
    )
```

time: 115 us -> 97.6 us (0.85)
  matrix products: 19.6 us -> 0 us
  Pallas kernels: 0 us -> 13.8 us
  local copies, waits for them, and re-layouts: 18.7 us -> 11.3 us
  other arithmetic: 6.2 us -> 0.56 us
  waiting for transfers between devices: 37.9 us -> 39.6 us
    dot_general x31 -> x0, matrix products: 19.6 us -> none  [the longest x5 3.84 us: body(): jnp.einsum('cgrk,rcgd->kcd', probs_low, d_attended, preferred_element_typ...]
    pallas_call x0 -> x5, Pallas kernels: none -> 13.8 us  [call(): pl.pallas_call(kernel, out_shape=[jax.ShapeDtypeStruct(shape, kind) for s...]
    unnamed x45 -> x48, local copies, waits for them, and re-layouts: 3.34 us -> 11.3 us
    gather x6 -> x0, local copies, waits for them, and re-layouts: 5.86 us -> none  [the longest x3 2.59 us: body(): slot_tiles = jnp.take_along_axis(plan_read, slot_order, axis=1)]
    transpose x4 -> x0, local copies, waits for them, and re-layouts: 5.73 us -> none  [body(): jnp.einsum('cgrk,rcgd->kcd', probs_low, d_attended, preferred_element_typ...]
    another operation x2 -> x0, local copies, waits for them, and re-layouts: 2.45 us -> none  [the longest x1 2.39 us: body(): jnp.stack(returns, axis=1).astype(jnp.bfloat16)]
    max x2 -> x0, other arithmetic: 2.16 us -> none  [the longest x1 2.15 us: body(): jnp.maximum(plan_given, 0)]
    all_to_all x2, waiting for transfers between devices: 37.9 us -> 39.6 us  [exchange(): lax.all_to_all(pieces, 'ctx', split_axis=0, concat_axis=0, tiled=True)]
  transfers between devices with their start and end apart: 2 -> 2, of which waited for: 2 -> 2; matrix products, arithmetic and copies ran while one was open for 11% -> 1% of each run, Pallas kernels for 0% -> 5%
where the time goes in v1:
time: 97.6 us; the launch traced here: 97 us
  waiting for transfers between devices  39.6 us (41%)
  starting transfers between devices  23.4 us (24%)
  Pallas kernels  13.8 us (14%)
  local copies, waits for them, and re-layouts  11.3 us (12%)
  blocking collectives  7.4 us (8%)
    all_to_all x2, waiting for transfers between devices, exchange(): lax.all_to_all(pieces, 'ctx', split_axis=0, concat_axis=0, tiled=True)  39.6 us
    all_to_all x2, starting transfers between devices, exchange(): lax.all_to_all(pieces, 'ctx', split_axis=0, concat_axis=0, tiled=True)  23.4 us
    pallas_call x5, Pallas kernels, call(): pl.pallas_call(kernel, out_shape=[jax.ShapeDtypeStruct(shape, kind) for s...  13.8 us
    unnamed x48, local copies, waits for them, and re-layouts  11.3 us
    all_gather x1, blocking collectives, body(): gate_sum = lax.all_gather(gate_part[0], 'head').sum(0)  7.4 us
  transfers between devices with their start and end apart: 2, of which 2 were waited for; matrix products, arithmetic and copies ran while one was open for 1% of the time, Pallas kernels for 5%

profile of v1, /device:TPU:6, one launch (start us, length us, event | category | flops | bytes accessed | tf_op | source)
XLA Modules:
  0.0 97.0 jit_solution(13388658970361919419)
XLA Ops:
  0.6 0.0 copy-start
  0.6 0.9 copy-done
  1.5 0.0 copy-start.4
  1.5 0.8 copy-done.4
  2.3 0.0 copy-start.6
  2.3 0.8 copy-done.6
  3.1 1.6 %send_kernel.1 = bf16[2048,256]{1,0:T(8,128)(2,1)} custom-call(s32[64,4,64]{2,1,0:T(4,128)S(1)} %copy-done, bf16[128,128]{1,0:T(8,128)(2,1)S(1)} %copy-done.4, bf16[128,128]{1,0:T(8,128)(2,1)S(1)} %copy-done.6), custom_call_target="tpu_custom_call" | custom-call | flops 134217728 | bytes 2097152 | tf_op jit(solution)/shard_map/send_kernel/pallas_call | solution.py:186
  4.6 0.0 copy-start.1
  4.6 0.0 copy-start.2
  4.6 0.0 copy-start.3
  4.6 0.0 copy-start.5
  4.6 0.0 copy-start.7
  4.6 0.0 copy-start.8
  4.7 16.7 %all-to-all-start = ((bf16[64,4,8,256]{3,2,1,0:T(8,128)(2,1)}), bf16[64,4,8,256]{3,2,1,0:T(8,128)(2,1)S(1)}, u32[]{:S(2)}, u32[]{:S(2)}) async-start(bf16[64,4,8,256]{3,2,1,0:T(8,128)(2,1)} %bitcast), calls=%async_computation | async-start | bytes 2097152 | tf_op jit(solution)/shard_map/all_to_all | solution.py:201
  21.4 0.0 copy-start.9
  21.4 0.0 copy-done.1
  21.4 0.0 copy-done.2
  21.4 0.0 copy-done.3
  21.4 0.0 copy-done.5
  21.4 0.0 copy-done.7
  21.5 0.0 copy-done.8
  21.5 0.6 copy-done.9
  22.1 0.6 local_kernel.1
  22.7 0.0 copy-start.14
  22.7 0.7 copy-done.14
  23.4 0.0 copy-start.17
  23.4 0.7 copy-done.17
  24.0 0.0 copy-start.10
  24.0 0.0 copy-start.12
  24.0 27.1 %all-to-all-done = bf16[64,4,8,256]{3,2,1,0:T(8,128)(2,1)S(1)} async-done(((bf16[64,4,8,256]{3,2,1,0:T(8,128)(2,1)}), bf16[64,4,8,256]{3,2,1,0:T(8,128)(2,1)S(1)}, u32[]{:S(2)}, u32[]{:S(2)}) %all-to-all-start) | async-done | bytes 1048608 | tf_op jit(solution)/shard_map/all_to_all | solution.py:201
  51.2 0.0 copy-start.15
  51.2 0.9 copy-done.15
  52.1 0.0 copy-start.18
  52.1 0.9 copy-done.18
  53.0 6.3 %main_kernel.1 = (bf16[2048,256]{1,0:T(8,128)(2,1)}, bf16[128,768]{1,0:T(8,128)(2,1)S(1)}, f32[8,768]{1,0:T(8,128)S(1)}) custom-call(bf16[2048,256]{1,0:T(8,128)(2,1)S(1)} %bitcast.7, bf16[128,768]{1,0:T(8,128)(2,1)S(1)} %get-tuple-element.19.query_t_ref, bf16[768,128]{1,0:T(8,128)(2,1)S(1)} %copy-done.15, bf16[128,768]{1,0:T(8,128)(2,1)S(1)} %copy-done.18, ...), custom_call_target="tpu_custom_call" | custom-call | flops 2147483648 | bytes 4194304 | tf_op jit(solution)/shard_map/main_kernel/pallas_call | solution.py:186
  59.3 0.0 copy-done.10
  59.3 0.0 copy-done.12
  59.3 0.0 copy-start.20
  59.3 0.7 copy-done.20
  60.0 0.0 copy-start.22
  60.0 0.0 copy-start.13
  60.0 0.0 copy-start.16
  60.0 0.6 copy-done.22
  60.6 6.7 %all-to-all-start.1 = ((bf16[64,4,8,256]{3,2,1,0:T(8,128)(2,1)}), bf16[64,4,8,256]{3,2,1,0:T(8,128)(2,1)S(1)}, u32[]{:S(2)}, u32[]{:S(2)}) async-start(bf16[64,4,8,256]{3,2,1,0:T(8,128)(2,1)} %bitcast.3), calls=%async_computation.1 | async-start | bytes 2097152 | tf_op jit(solution)/shard_map/all_to_all | solution.py:201
  67.3 0.0 copy-done.13
  67.3 0.0 copy-done.16
  67.3 0.0 copy-start.11
  67.3 1.2 %copy-done.11 = f32[2048,128]{1,0:T(8,128)S(1)} copy-done((f32[2048,128]{1,0:T(8,128)S(1)}, f32[2048,128]{1,0:T(8,128)}, u32[]{:S(2)}) %copy-start.11) | copy-done | bytes 1048600
  68.6 0.0 copy-start.19
  68.6 0.9 copy-done.19
  69.5 0.0 copy-start.21
  69.5 0.9 copy-done.21
  70.4 0.0 copy-start.23
  70.4 0.7 copy-done.23
  71.1 4.4 %query_kernel.1 = (bf16[128,768]{1,0:T(8,128)(2,1)}, f32[128,256]{1,0:T(8,128)S(1)}, f32[1,128]{1,0:T(1,128)S(1)}, bf16[128,2048]{1,0:T(8,128)(2,1)S(1)}) custom-call(s32[64,4,64]{2,1,0:T(4,128)S(1)} %copy-done.1, bf16[2048,256]{1,0:T(8,128)(2,1)S(1)} %bitcast.8, bf16[128,128]{1,0:T(8,128)(2,1)S(1)} %copy-done.5, bf16[128,128]{1,0:T(8,128)(2,1)S(1)} %copy-done.7, ...), custom_call_target="tpu_custom_call" | custom-call | flops 2147483648 | bytes 4194304 | tf_op jit(solution)/shard_map/query_kernel/pallas_call | solution.py:186
  75.5 7.4 %all-gather = f32[8,1,128]{2,1,0:T(1,128)S(1)} all-gather(f32[1,1,128]{2,1,0:T(1,128)S(1)} %bitcast.9), channel_id=1, replica_groups=mesh['head'=8,'ctx'=64] {'head'}, dimensions={0}, use_global_device_ids=true | all-gather | bytes 4608 | tf_op jit(solution)/shard_map/all_gather | solution.py:234
  83.0 0.5 fusion
  83.5 12.5 %all-to-all-done.1 = bf16[64,4,8,256]{3,2,1,0:T(8,128)(2,1)S(1)} async-done(((bf16[64,4,8,256]{3,2,1,0:T(8,128)(2,1)}), bf16[64,4,8,256]{3,2,1,0:T(8,128)(2,1)S(1)}, u32[]{:S(2)}, u32[]{:S(2)}) %all-to-all-start.1) | async-done | bytes 1048608 | tf_op jit(solution)/shard_map/all_to_all | solution.py:201
  96.0 0.9 owner_kernel.1
  (1 shorter events, 0.0 us)
Async XLA Ops:
  0.6 0.9 copy-start
  1.5 0.8 copy-start.4
  2.3 0.8 copy-start.6
  4.6 16.8 %copy-start.1 = (s32[64,4,64]{2,1,0:T(4,128)S(1)}, s32[64,4,64]{2,1,0:T(4,128)}, u32[]{:S(2)}) copy-start(s32[64,4,64]{2,1,0:T(4,128)} %plan_ref.5) | copy-start | bytes 196612
  4.6 16.8 %copy-start.2 = (bf16[128,768]{1,0:T(8,128)(2,1)S(1)}, bf16[128,768]{1,0:T(8,128)(2,1)}, u32[]{:S(2)}) copy-start(bf16[128,768]{1,0:T(8,128)(2,1)} %query_ref.1) | copy-start | bytes 589828
  4.6 16.8 %copy-start.3 = (bf16[128,768]{1,0:T(8,128)(2,1)S(1)}, bf16[128,768]{1,0:T(8,128)(2,1)}, u32[]{:S(2)}) copy-start(bf16[128,768]{1,0:T(8,128)(2,1)} %grad_ref.3) | copy-start | bytes 589828
  4.6 16.8 %copy-start.5 = (bf16[128,128]{1,0:T(8,128)(2,1)S(1)}, bf16[128,128]{1,0:T(8,128)(2,1)}, u32[]{:S(2)}) copy-start(bf16[128,128]{1,0:T(8,128)(2,1)} %key_ref.5) | copy-start | bytes 98308
  4.6 16.8 %copy-start.7 = (bf16[128,128]{1,0:T(8,128)(2,1)S(1)}, bf16[128,128]{1,0:T(8,128)(2,1)}, u32[]{:S(2)}) copy-start(bf16[128,128]{1,0:T(8,128)(2,1)} %value_ref.5) | copy-start | bytes 98308
  4.6 16.8 %copy-start.8 = (s32[1,4,64]{2,1,0:T(4,128)S(1)}, s32[1,4,64]{2,1,0:T(4,128)}, u32[]{:S(2)}) copy-start(s32[1,4,64]{2,1,0:T(4,128)} %kind_ref.1) | copy-start | bytes 3076
  4.7 46.5 %all-to-all-start = ((bf16[64,4,8,256]{3,2,1,0:T(8,128)(2,1)}), bf16[64,4,8,256]{3,2,1,0:T(8,128)(2,1)S(1)}, u32[]{:S(2)}, u32[]{:S(2)}) async-start(bf16[64,4,8,256]{3,2,1,0:T(8,128)(2,1)} %bitcast), calls=%async_computation | async-start | bytes 2097152 | tf_op jit(solution)/shard_map/all_to_all | solution.py:201
  21.4 0.7 copy-start.9
  22.7 0.7 copy-start.14
  23.4 0.7 copy-start.17
  24.0 35.3 %copy-start.10 = (f32[2048,128]{1,0:T(8,128)}, f32[2048,128]{1,0:T(8,128)S(1)}, u32[]{:S(2)}) copy-start(f32[2048,128]{1,0:T(8,128)S(1)} %get-tuple-element.22.bias_ref) | copy-start | bytes 3145732
  24.0 35.3 %copy-start.12 = (bf16[128,768]{1,0:T(8,128)(2,1)}, bf16[128,768]{1,0:T(8,128)(2,1)S(1)}, u32[]{:S(2)}) copy-start(bf16[128,768]{1,0:T(8,128)(2,1)S(1)} %get-tuple-element.19.query_t_ref) | copy-start | bytes 589828
  51.2 0.9 copy-start.15
  52.1 0.9 copy-start.18
  59.3 0.7 copy-start.20
  60.0 0.6 copy-start.22
  60.0 7.3 %copy-start.13 = (bf16[128,768]{1,0:T(8,128)(2,1)S(1)}, bf16[128,768]{1,0:T(8,128)(2,1)}, u32[]{:S(2)}) copy-start(bf16[128,768]{1,0:T(8,128)(2,1)} %copy-done.12) | copy-start | bytes 589828
  60.0 7.3 %copy-start.16 = (bf16[768,128]{1,0:T(8,128)(2,1)S(1)}, bf16[768,128]{1,0:T(8,128)(2,1)}, u32[]{:S(2)}) copy-start(bf16[768,128]{1,0:T(8,128)(2,1)} %copy-done.14) | copy-start | bytes 589828
  60.6 35.4 %all-to-all-start.1 = ((bf16[64,4,8,256]{3,2,1,0:T(8,128)(2,1)}), bf16[64,4,8,256]{3,2,1,0:T(8,128)(2,1)S(1)}, u32[]{:S(2)}, u32[]{:S(2)}) async-start(bf16[64,4,8,256]{3,2,1,0:T(8,128)(2,1)} %bitcast.3), calls=%async_computation.1 | async-start | bytes 2097152 | tf_op jit(solution)/shard_map/all_to_all | solution.py:201
  67.3 1.2 %copy-start.11 = (f32[2048,128]{1,0:T(8,128)S(1)}, f32[2048,128]{1,0:T(8,128)}, u32[]{:S(2)}) copy-start(f32[2048,128]{1,0:T(8,128)} %copy-done.10) | copy-start | bytes 3145732
  68.6 0.9 copy-start.19
  69.5 0.9 copy-start.21
  70.4 0.7 copy-start.23

commit v2 on v1

v2 whole, which is shorter than its diff:
```python
import math

import jax
import jax.numpy as jnp
from jax import lax
from jax.experimental import pallas as pl
from jax.experimental.pallas import tpu as pltpu
from jax.sharding import PartitionSpec as P

HD = 128
TILE = 8
SECTIONS = 4
ROWS = 128
PEERS = 64
GROUP = 6
SLOTS = PEERS * SECTIONS
KEYS = SLOTS * TILE
PICKS = 32
KEPT = SECTIONS * PICKS
NEAR = KEPT * TILE
WIDE = GROUP * ROWS
CHUNK = 256
N_CHUNK = NEAR // CHUNK
SEND_PARTS = 4
FACTOR = 1.0 / math.sqrt(HD)
SCALE = FACTOR * math.log2(math.e)
HIDDEN = -1e30
INTERPRET = False
VMEM_LIMIT = 16 * 1024 * 1024

f32 = jnp.float32
bf16 = jnp.bfloat16


def dot(a, b):
    return lax.dot_general(a, b, (((1,), (0,)), ((), ())), preferred_element_type=f32)


def head(h):
    return slice(h * HD, (h + 1) * HD)


def owner_tiles(plan_ref, slot_ref, device):
    for b in range(PEERS):
        slot_ref[b * SECTIONS : (b + 1) * SECTIONS, :] = plan_ref[b].astype(f32)
    pick = (lax.broadcasted_iota(jnp.int32, (PEERS, HD), 0) == device).astype(bf16)
    return dot(slot_ref[...].astype(bf16), pick)


def owner_matrix(tiles):
    column = lax.broadcasted_iota(jnp.int32, (TILE, HD), 1)
    row = lax.broadcasted_iota(jnp.int32, (TILE, HD), 0)
    wanted = jnp.where((column & (TILE - 1)) == row, (column >> 3).astype(f32), -2.0)
    slots = tiles.shape[0]
    wide = jnp.broadcast_to(tiles[:, None, :], (slots, TILE, HD))
    return jnp.where(wide == wanted[None], 1.0, 0.0).reshape(slots * TILE, HD).astype(bf16)


def send_kernel(plan_hbm, key_hbm, value_hbm, out_hbm, plan_ref, key_ref, value_ref, out_ref, slot_ref, sems):
    loads = [
        pltpu.make_async_copy(plan_hbm, plan_ref, sems.at[0]),
        pltpu.make_async_copy(key_hbm, key_ref, sems.at[1]),
        pltpu.make_async_copy(value_hbm, value_ref, sems.at[2]),
    ]
    for load in loads:
        load.start()
    for load in loads:
        load.wait()
    tiles = owner_tiles(plan_ref, slot_ref, lax.axis_index("ctx"))
    both = jnp.concatenate([key_ref[...], value_ref[...]], axis=1)
    stores = []
    for c in range(SEND_PARTS):
        size = KEYS // SEND_PARTS
        matrix = owner_matrix(tiles[c * size // TILE : (c + 1) * size // TILE])
        out_ref[c * size : (c + 1) * size, :] = dot(matrix, both).astype(bf16)
        part = pl.ds(c * size, size)
        stores.append(pltpu.make_async_copy(out_ref.at[part], out_hbm.at[part], sems.at[3 + c]))
        stores[-1].start()
    for store in stores:
        store.wait()


def row_gate(logit_ref):
    return jax.nn.sigmoid(logit_ref[...])


def causal_scores(key_ref, query_t):
    scores = dot(key_ref[...], query_t)
    key_at = lax.broadcasted_iota(jnp.int32, (ROWS, WIDE), 0)
    row_at = lax.broadcasted_iota(jnp.int32, (ROWS, WIDE), 1) & (ROWS - 1)
    return jnp.where(row_at >= key_at, scores, HIDDEN)


def local_kernel(
    plan_ref, kind_ref, query_ref, key_ref, value_ref, grad_ref, logit_ref,
    query_t_ref, query_s_ref, d_att_t_ref, bias_ref, start_ref, out_t_ref, list_ref,
):
    gate = row_gate(logit_ref)
    for h in range(GROUP):
        block = query_ref[:, head(h)]
        query_s_ref[head(h), :] = block
        query_t_ref[:, head(h)] = block.astype(f32).T.astype(bf16)
        grad_t = grad_ref[:, head(h)].astype(f32).T
        d_att_t_ref[:, head(h)] = (gate * grad_t).astype(bf16)
    scores = causal_scores(key_ref, query_t_ref[...])
    top = jnp.max(scores, axis=0, keepdims=True)
    weights = jnp.exp2((scores - top) * SCALE)
    start_ref[0:1, :] = top
    start_ref[1:2, :] = jnp.sum(weights, axis=0, keepdims=True)
    value_t = value_ref[...].astype(f32).T.astype(bf16)
    out_t_ref[...] = dot(value_t, weights.astype(bf16))
    device = lax.axis_index("ctx")
    bias_ref[...] = jnp.full((NEAR, HD), HIDDEN, f32)
    late = lax.broadcasted_iota(jnp.int32, (TILE, HD), 1) >= ROWS // 2
    for s in range(SECTIONS):

        @pl.loop(0, PICKS)
        def _(k):
            list_ref[s * PICKS + k] = device * SECTIONS + s

        def place(p, count):
            given = plan_ref[s, p] >= 0

            @pl.when(given)
            def _():
                list_ref[s * PICKS + count] = p * SECTIONS + s
                at = pl.multiple_of((s * PICKS + count) * TILE, TILE)
                floor = jnp.where(kind_ref[s, p] == 0, 0.0, HIDDEN)
                bias_ref[pl.ds(at, TILE), :] = jnp.where(late, 0.0, floor)

            return count + given.astype(jnp.int32)

        lax.fori_loop(0, PEERS, place, jnp.int32(0))


def gather_tiles(list_ref, slots_ref, near_ref):
    for k in range(KEPT):
        near_ref[k * TILE : (k + 1) * TILE, :] = slots_ref[list_ref[k]]


def main_kernel(
    list_ref, slots_ref, query_t_ref, bias_ref, start_ref, query_s_hbm, d_att_t_hbm, out_t_hbm,
    grad_hbm, att_t_hbm, stat_hbm,
    kv_ref, grad_ref, score_ref, weight_ref, query_s_ref, d_att_t_ref, out_t_ref, att_t_ref, stat_ref, sems,
):
    loads = [
        pltpu.make_async_copy(query_s_hbm, query_s_ref, sems.at[0]),
        pltpu.make_async_copy(d_att_t_hbm, d_att_t_ref, sems.at[1]),
        pltpu.make_async_copy(out_t_hbm, out_t_ref, sems.at[2]),
    ]
    for load in loads:
        load.start()
    gather_tiles(list_ref, slots_ref, kv_ref)
    grad_ref[...] = jnp.zeros_like(grad_ref)
    top = jnp.broadcast_to(start_ref[0:1, :], (TILE, WIDE))
    for c in range(N_CHUNK):
        rows = slice(c * CHUNK, (c + 1) * CHUNK)
        scores = dot(kv_ref[rows, :HD], query_t_ref[...])
        scores = scores + jnp.concatenate([bias_ref[rows, :]] * GROUP, axis=1)
        score_ref[rows, :] = scores
        top = jnp.maximum(top, jnp.max(scores.reshape(CHUNK // TILE, TILE, WIDE), axis=0))
    top = jnp.max(top, axis=0, keepdims=True)
    total = jnp.zeros((TILE, WIDE), f32)
    out_t = jnp.zeros((HD, WIDE), f32)
    for c in range(N_CHUNK):
        rows = slice(c * CHUNK, (c + 1) * CHUNK)
        weights = jnp.exp2((score_ref[rows, :] - top) * SCALE)
        total = total + jnp.sum(weights.reshape(CHUNK // TILE, TILE, WIDE), axis=0)
        low = weights.astype(bf16)
        weight_ref[rows, :] = low
        out_t = out_t + dot(kv_ref[rows, HD:].T, low)
    share = jnp.exp2((start_ref[0:1, :] - top) * SCALE)
    total = jnp.sum(total, axis=0, keepdims=True) + share * start_ref[1:2, :]
    inverse = 1.0 / total
    for load in loads:
        load.wait()
    att_t = ((out_t + share * out_t_ref[...]) * inverse).astype(bf16)
    att_t_ref[...] = att_t
    d_att_t = d_att_t_ref[...].astype(f32)
    delta = jnp.sum(d_att_t * att_t.astype(f32), axis=0, keepdims=True) * inverse
    d_low_t = (d_att_t * inverse).astype(bf16)
    d_low_s = jnp.concatenate([d_low_t[:, head(h)].T for h in range(GROUP)], axis=0)
    stat_ref[0:1, :] = top
    stat_ref[1:2, :] = inverse
    stat_ref[2:3, :] = delta
    stores = [
        pltpu.make_async_copy(att_t_ref, att_t_hbm, sems.at[3]),
        pltpu.make_async_copy(stat_ref, stat_hbm, sems.at[4]),
    ]

    def scatter(values, c, side):
        for k in range(CHUNK // TILE):
            slot = list_ref[c * (CHUNK // TILE) + k]
            grad_ref[slot, :, side * HD : (side + 1) * HD] = values[k * TILE : (k + 1) * TILE, :]

    def send(side):
        half = pl.ds(side * HD, HD)
        stores.append(
            pltpu.make_async_copy(grad_ref.at[:, :, half], grad_hbm.at[:, :, half], sems.at[5 + side])
        )
        stores[-1].start()

    for store in stores:
        store.start()
    for c in range(N_CHUNK):
        rows = slice(c * CHUNK, (c + 1) * CHUNK)
        scatter(dot(weight_ref[rows, :], d_low_s).astype(bf16), c, 1)
    send(1)
    for c in range(N_CHUNK):
        rows = slice(c * CHUNK, (c + 1) * CHUNK)
        d_probs = dot(kv_ref[rows, HD:], d_low_t)
        d_scores = (weight_ref[rows, :].astype(f32) * (d_probs - delta)).astype(bf16)
        scatter((dot(d_scores, query_s_ref[...]) * FACTOR).astype(bf16), c, 0)
    send(0)
    for store in stores:
        store.wait()


def query_kernel(
    list_ref, plan_ref, slots_ref, key_ref, value_ref, grad_ref, query_t_ref, query_s_ref, d_att_t_ref, bias_ref,
    att_t_ref, stat_ref, query_grad_ref, local_ref, gate_ref, owner_ref, slot_ref, kv_ref,
):
    gather_tiles(list_ref, slots_ref, kv_ref)
    top, inverse, delta = stat_ref[0:1, :], stat_ref[1:2, :], stat_ref[2:3, :]
    d_low_t = (d_att_t_ref[...].astype(f32) * inverse).astype(bf16)
    d_low_s = jnp.concatenate([d_low_t[:, head(h)].T for h in range(GROUP)], axis=0)

    def d_score(scores, values):
        weights = jnp.exp2((scores - top) * SCALE)
        d_scores = (weights * (dot(values, d_low_t) - delta)).astype(bf16)
        return weights.astype(bf16), d_scores

    weights, d_scores = d_score(causal_scores(key_ref, query_t_ref[...]), value_ref[...])
    local_ref[:, :HD] = dot(d_scores, query_s_ref[...]) * FACTOR
    local_ref[:, HD:] = dot(weights, d_low_s)
    total = dot(key_ref[...].T, d_scores)
    for c in range(N_CHUNK):
        rows = slice(c * CHUNK, (c + 1) * CHUNK)
        keys = kv_ref[rows, :HD]
        scores = dot(keys, query_t_ref[...]) + jnp.concatenate([bias_ref[rows, :]] * GROUP, axis=1)
        _, d_scores = d_score(scores, kv_ref[rows, HD:])
        total = total + dot(keys.T, d_scores)
    part = jnp.zeros((1, ROWS), f32)
    for h in range(GROUP):
        query_grad_ref[:, head(h)] = (total[:, head(h)] * FACTOR).T.astype(bf16)
        grad_t = grad_ref[:, head(h)].astype(f32).T
        part = part + jnp.sum(grad_t * att_t_ref[:, head(h)].astype(f32), axis=0, keepdims=True)
    gate_ref[...] = part
    matrix = owner_matrix(owner_tiles(plan_ref, slot_ref, lax.axis_index("ctx")))
    for c in range(KEYS // HD):
        owner_ref[:, c * HD : (c + 1) * HD] = matrix[c * HD : (c + 1) * HD, :].T


def owner_kernel(owner_ref, returned_ref, local_ref, key_grad_ref, value_grad_ref):
    total = local_ref[...] + dot(owner_ref[...], returned_ref[...])
    key_grad_ref[...] = total[:, :HD].astype(bf16)
    value_grad_ref[...] = total[:, HD:].astype(bf16)


VMEM = pltpu.VMEM
SMEM = pltpu.SMEM
HBM = pltpu.HBM


def call(kernel, ins, outs, scratch, flops, moved, limit=VMEM_LIMIT):
    return pl.pallas_call(
        kernel,
        out_shape=[jax.ShapeDtypeStruct(shape, kind) for _, shape, kind in outs],
        in_specs=[pl.BlockSpec(memory_space=space) for space, _ in ins],
        out_specs=[pl.BlockSpec(memory_space=space) for space, _, _ in outs],
        scratch_shapes=scratch,
        compiler_params=pltpu.CompilerParams(vmem_limit_bytes=limit),
        cost_estimate=pl.CostEstimate(flops=flops, bytes_accessed=moved, transcendentals=0),
        interpret=INTERPRET,
        name=kernel.__name__,
    )(*[array for _, array in ins])


def exchange(pieces):
    return lax.all_to_all(pieces, "ctx", split_axis=0, concat_axis=0, tiled=True)


def body(queries, key_rows, value_rows, out_grad, gate_logit, tile_plan, mask_kind):
    logit = gate_logit.reshape(1, ROWS)
    plan_row = lax.dynamic_index_in_dim(tile_plan, lax.axis_index("ctx"), 0, keepdims=False)
    (outgoing,) = call(
        send_kernel,
        [(HBM, tile_plan), (HBM, key_rows), (HBM, value_rows)],
        [(HBM, (KEYS, 2 * HD), bf16)],
        [VMEM((PEERS, SECTIONS, PEERS), jnp.int32), VMEM((ROWS, HD), bf16), VMEM((ROWS, HD), bf16),
         VMEM((KEYS, 2 * HD), bf16),
         VMEM((SLOTS, PEERS), f32), pltpu.SemaphoreType.DMA((3 + SEND_PARTS,))],
        2**27, 2**21, limit=None,
    )
    fetched = exchange(outgoing.reshape(PEERS, SECTIONS, TILE, 2 * HD)).reshape(SLOTS, TILE, 2 * HD)
    query_t, query_s, d_att_t, bias, start, out_t, places = call(
        local_kernel,
        [(SMEM, plan_row), (SMEM, mask_kind[0]), (VMEM, queries), (VMEM, key_rows), (VMEM, value_rows),
         (VMEM, out_grad), (VMEM, logit)],
        [(VMEM, (HD, WIDE), bf16), (VMEM, (WIDE, HD), bf16), (VMEM, (HD, WIDE), bf16), (VMEM, (NEAR, HD), f32),
         (VMEM, (8, WIDE), f32), (VMEM, (HD, WIDE), f32), (SMEM, (KEPT,), jnp.int32)],
        [], 2**27, 2**22,
    )
    grads, att_t, stat = call(
        main_kernel,
        [(SMEM, places), (VMEM, fetched), (VMEM, query_t), (VMEM, bias), (VMEM, start),
         (HBM, query_s), (HBM, d_att_t), (HBM, out_t)],
        [(HBM, (SLOTS, TILE, 2 * HD), bf16), (HBM, (HD, WIDE), bf16), (HBM, (8, WIDE), f32)],
        [VMEM((NEAR, 2 * HD), bf16), VMEM((SLOTS, TILE, 2 * HD), bf16), VMEM((NEAR, WIDE), f32), VMEM((NEAR, WIDE), bf16),
         VMEM((WIDE, HD), bf16), VMEM((HD, WIDE), bf16), VMEM((HD, WIDE), f32), VMEM((HD, WIDE), bf16),
         VMEM((8, WIDE), f32), pltpu.SemaphoreType.DMA((7,))],
        2**30, 2**22,
    )
    returned = exchange(grads.reshape(PEERS, SECTIONS, TILE, 2 * HD)).reshape(KEYS, 2 * HD)
    query_grad, local, gate_part, owner = call(
        query_kernel,
        [(SMEM, places), (VMEM, tile_plan), (VMEM, fetched), (VMEM, key_rows), (VMEM, value_rows), (VMEM, out_grad),
         (VMEM, query_t), (VMEM, query_s), (VMEM, d_att_t), (VMEM, bias), (VMEM, att_t), (VMEM, stat)],
        [(VMEM, (ROWS, WIDE), bf16), (VMEM, (ROWS, 2 * HD), f32), (VMEM, (1, ROWS), f32), (VMEM, (HD, KEYS), bf16)],
        [VMEM((SLOTS, PEERS), f32), VMEM((NEAR, 2 * HD), bf16)],
        2**30, 2**22,
    )
    gate = jax.nn.sigmoid(gate_logit)
    gate_sum = lax.all_gather(gate_part[0], "head").sum(0)
    gate_grad = gate * (1.0 - gate) * gate_sum
    key_grad, value_grad = call(
        owner_kernel,
        [(VMEM, owner), (VMEM, returned), (VMEM, local)],
        [(VMEM, (ROWS, HD), bf16), (VMEM, (ROWS, HD), bf16)],
        [], 2**27, 2**21,
    )
    return (query_grad, key_grad, value_grad, gate_grad)


def solution(mesh):
    placed = (
        P("ctx", "head"),
        P("ctx", "head"),
        P("ctx", "head"),
        P("ctx", "head"),
        P("ctx"),
        P(),
        P("ctx", None, None),
    )
    return jax.shard_map(
        body,
        mesh=mesh,
        in_specs=placed,
        out_specs=(P("ctx", "head"), P("ctx", "head"), P("ctx", "head"), P("ctx")),
        check_vma=False,
    )
```

time: 97.6 us -> 93.6 us (0.959)
  Pallas kernels: 13.8 us -> 19.6 us
  local copies, waits for them, and re-layouts: 11.3 us -> 5.58 us
  waiting for transfers between devices: 39.6 us -> 35.9 us
    pallas_call x5, Pallas kernels: 13.8 us -> 19.6 us  [call(): pl.pallas_call(kernel, out_shape=[jax.ShapeDtypeStruct(shape, kind) for _...]
    unnamed x48 -> x30, local copies, waits for them, and re-layouts: 11.3 us -> 5.57 us
    all_to_all x2, waiting for transfers between devices: 39.6 us -> 35.9 us  [exchange(): lax.all_to_all(pieces, 'ctx', split_axis=0, concat_axis=0, tiled=True)]
  transfers between devices with their start and end apart: 2 -> 2, of which waited for: 2 -> 2; matrix products, arithmetic and copies ran while one was open for 1% -> 1% of each run, Pallas kernels for 5% -> 11%
where the time goes in v2:
time: 93.6 us; the launch traced here: 93.1 us
  waiting for transfers between devices  35.9 us (38%)
  starting transfers between devices  23.2 us (25%)
  Pallas kernels  19.6 us (21%)
  blocking collectives  7.39 us (8%)
  local copies, waits for them, and re-layouts  5.58 us (6%)
    all_to_all x2, waiting for transfers between devices, exchange(): lax.all_to_all(pieces, 'ctx', split_axis=0, concat_axis=0, tiled=True)  35.9 us
    all_to_all x2, starting transfers between devices, exchange(): lax.all_to_all(pieces, 'ctx', split_axis=0, concat_axis=0, tiled=True)  23.2 us
    pallas_call x5, Pallas kernels, call(): pl.pallas_call(kernel, out_shape=[jax.ShapeDtypeStruct(shape, kind) for _...  19.6 us
    all_gather x1, blocking collectives, body(): gate_sum = lax.all_gather(gate_part[0], 'head').sum(0)  7.39 us
    unnamed x30, local copies, waits for them, and re-layouts  5.57 us
  transfers between devices with their start and end apart: 2, of which 2 were waited for; matrix products, arithmetic and copies ran while one was open for 1% of the time, Pallas kernels for 11%

profile of v2, /device:TPU:6, one launch (start us, length us, event | category | flops | bytes accessed | tf_op | source)
XLA Modules:
  0.0 93.1 jit_solution(8147312617758026968)
XLA Ops:
  0.6 2.4 %send_kernel.1 = bf16[2048,256]{1,0:T(8,128)(2,1)} custom-call(s32[64,4,64]{2,1,0:T(4,128)} %plan_ref.1, bf16[128,128]{1,0:T(8,128)(2,1)} %key_ref.3, bf16[128,128]{1,0:T(8,128)(2,1)} %value_ref.3), custom_call_target="tpu_custom_call" | custom-call | flops 134217728 | bytes 2097152 | tf_op jit(solution)/shard_map/send_kernel/pallas_call | solution.py:266
  3.0 0.0 copy-start
  3.0 0.0 copy-start.1
  3.0 0.0 copy-start.2
  3.1 0.0 copy-start.3
  3.1 0.0 copy-start.4
  3.1 16.7 %all-to-all-start = ((bf16[64,4,8,256]{3,2,1,0:T(8,128)(2,1)}), bf16[64,4,8,256]{3,2,1,0:T(8,128)(2,1)S(1)}, u32[]{:S(2)}, u32[]{:S(2)}) async-start(bf16[64,4,8,256]{3,2,1,0:T(8,128)(2,1)} %bitcast.15), calls=%async_computation | async-start | bytes 2097152 | tf_op jit(solution)/shard_map/all_to_all | solution.py:280
  19.8 0.0 copy-done
  19.8 0.0 copy-start.5
  19.9 0.0 copy-start.6
  19.9 0.0 copy-done.1
  19.9 0.0 copy-done.2
  19.9 0.0 copy-done.3
  19.9 0.0 copy-done.4
  19.9 0.6 copy-done.5
  20.5 0.0 copy-done.6
  20.5 7.0 %local_kernel.1 = (bf16[128,768]{1,0:T(8,128)(2,1)S(1)}, bf16[768,128]{1,0:T(8,128)(2,1)S(1)}, bf16[128,768]{1,0:T(8,128)(2,1)S(1)}, f32[1024,128]{1,0:T(8,128)S...) custom-call(s32[4,64]{1,0:T(4,128)S(1)} %dynamic-slice_bitcast_fusion.plan_ref, ...), custom_call_target="tpu_custom_call" | custom-call | flops 134217728 | bytes 4194304 | tf_op jit(solution)/shard_map/local_kernel/pallas_call | solution.py:266
  27.6 0.0 copy-start.7
  27.6 0.0 copy-start.9
  27.6 22.0 %all-to-all-done = bf16[64,4,8,256]{3,2,1,0:T(8,128)(2,1)S(1)} async-done(((bf16[64,4,8,256]{3,2,1,0:T(8,128)(2,1)}), bf16[64,4,8,256]{3,2,1,0:T(8,128)(2,1)S(1)}, u32[]{:S(2)}, u32[]{:S(2)}) %all-to-all-start) | async-done | bytes 1048608 | tf_op jit(solution)/shard_map/all_to_all | solution.py:280
  49.6 5.8 %main_kernel.1 = (bf16[256,8,256]{2,1,0:T(8,128)(2,1)}, bf16[128,768]{1,0:T(8,128)(2,1)S(1)}, f32[8,768]{1,0:T(8,128)S(1)}) custom-call(s32[128]{0:T(128)S(1)} %get-tuple-element.20.list_ref, bf16[256,8,256]{2,1,0:T(8,128)(2,1)S(1)} %bitcast.10, bf16[128,768]{1,0:T(8,128)(2,1)S(1)} %get-tuple-element.21.query_t_ref, ...), custom_call_target="tpu_custom_call" | custom-call | flops 1073741824 | bytes 4194304 | tf_op jit(solution)/shard_map/main_kernel/pallas_call | solution.py:266
  55.4 0.0 copy-done.7
  55.4 0.0 copy-done.9
  55.5 0.0 copy-start.11
  55.5 0.7 copy-done.11
  56.1 0.0 copy-start.13
  56.1 0.6 copy-done.13
  56.7 6.5 %all-to-all-start.1 = ((bf16[64,4,8,256]{3,2,1,0:T(8,128)(2,1)}), bf16[64,4,8,256]{3,2,1,0:T(8,128)(2,1)S(1)}, u32[]{:S(2)}, u32[]{:S(2)}) async-start(bf16[64,4,8,256]{3,2,1,0:T(8,128)(2,1)} %bitcast.5), calls=%async_computation.1 | async-start | bytes 2097152 | tf_op jit(solution)/shard_map/all_to_all | solution.py:280
  63.2 0.0 copy-start.8
  63.2 1.0 %copy-done.8 = f32[1024,128]{1,0:T(8,128)S(1)} copy-done((f32[1024,128]{1,0:T(8,128)S(1)}, f32[1024,128]{1,0:T(8,128)}, u32[]{:S(2)}) %copy-start.8) | copy-done | bytes 524312
  64.3 0.0 copy-start.10
  64.3 0.9 copy-done.10
  65.2 0.0 copy-start.12
  65.2 0.9 copy-done.12
  66.1 0.0 copy-start.14
  66.1 0.7 copy-done.14
  66.9 3.4 %query_kernel.1 = (bf16[128,768]{1,0:T(8,128)(2,1)}, f32[128,256]{1,0:T(8,128)S(1)}, f32[1,128]{1,0:T(1,128)S(1)}, bf16[128,2048]{1,0:T(8,128)(2,1)S(1)}) custom-call(s32[128]{0:T(128)S(1)} %get-tuple-element.20.list_ref, s32[64,4,64]{2,1,0:T(4,128)S(1)} %copy-done, bf16[256,8,256]{2,1,0:T(8,128)(2,1)S(1)} %bitcast.11, bf16[128,128]{1,0:T(8,128)(2,1)S(1)} %copy-done.1, ...), custom_call_target="tpu_custom_call" | custom-call | flops 1073741824 | bytes 4194304 | tf_op jit(solution)/shard_map/query_kernel/pallas_call | solution.py:266
  70.3 7.4 %all-gather = f32[8,1,128]{2,1,0:T(1,128)S(1)} all-gather(f32[1,1,128]{2,1,0:T(1,128)S(1)} %bitcast.12), channel_id=1, replica_groups=mesh['head'=8,'ctx'=64] {'head'}, dimensions={0}, use_global_device_ids=true | all-gather | bytes 4608 | tf_op jit(solution)/shard_map/all_gather | solution.py:324
  77.7 0.5 fusion
  78.2 13.9 %all-to-all-done.1 = bf16[64,4,8,256]{3,2,1,0:T(8,128)(2,1)S(1)} async-done(((bf16[64,4,8,256]{3,2,1,0:T(8,128)(2,1)}), bf16[64,4,8,256]{3,2,1,0:T(8,128)(2,1)S(1)}, u32[]{:S(2)}, u32[]{:S(2)}) %all-to-all-start.1) | async-done | bytes 1048608 | tf_op jit(solution)/shard_map/all_to_all | solution.py:280
  92.1 0.9 %owner_kernel.1 = (bf16[128,128]{1,0:T(8,128)(2,1)}, bf16[128,128]{1,0:T(8,128)(2,1)}) custom-call(bf16[128,2048]{1,0:T(8,128)(2,1)S(1)} %get-tuple-element.30.owner_ref, bf16[2048,256]{1,0:T(8,128)(2,1)S(1)} %bitcast.9, f32[128,256]{1,0:T(8,128)S(1)} %get-tuple-element.32.local_ref), custom_call_target="tpu_custom_call" | custom-call | flops 134217728 | bytes 2097152 | tf_op jit(solution)/shard_map/owner_kernel/pallas_call | solution.py:266
  (2 shorter events, 0.0 us)
Async XLA Ops:
  3.0 16.8 %copy-start = (s32[64,4,64]{2,1,0:T(4,128)S(1)}, s32[64,4,64]{2,1,0:T(4,128)}, u32[]{:S(2)}) copy-start(s32[64,4,64]{2,1,0:T(4,128)} %plan_ref.1) | copy-start | bytes 196612
  3.0 16.8 %copy-start.1 = (bf16[128,128]{1,0:T(8,128)(2,1)S(1)}, bf16[128,128]{1,0:T(8,128)(2,1)}, u32[]{:S(2)}) copy-start(bf16[128,128]{1,0:T(8,128)(2,1)} %key_ref.3) | copy-start | bytes 98308
  3.0 16.8 %copy-start.2 = (bf16[128,128]{1,0:T(8,128)(2,1)S(1)}, bf16[128,128]{1,0:T(8,128)(2,1)}, u32[]{:S(2)}) copy-start(bf16[128,128]{1,0:T(8,128)(2,1)} %value_ref.3) | copy-start | bytes 98308
  3.1 16.8 %copy-start.3 = (bf16[128,768]{1,0:T(8,128)(2,1)S(1)}, bf16[128,768]{1,0:T(8,128)(2,1)}, u32[]{:S(2)}) copy-start(bf16[128,768]{1,0:T(8,128)(2,1)} %query_ref.1) | copy-start | bytes 589828
  3.1 16.8 %copy-start.4 = (bf16[128,768]{1,0:T(8,128)(2,1)S(1)}, bf16[128,768]{1,0:T(8,128)(2,1)}, u32[]{:S(2)}) copy-start(bf16[128,768]{1,0:T(8,128)(2,1)} %grad_ref.3) | copy-start | bytes 589828
  3.1 46.5 %all-to-all-start = ((bf16[64,4,8,256]{3,2,1,0:T(8,128)(2,1)}), bf16[64,4,8,256]{3,2,1,0:T(8,128)(2,1)S(1)}, u32[]{:S(2)}, u32[]{:S(2)}) async-start(bf16[64,4,8,256]{3,2,1,0:T(8,128)(2,1)} %bitcast.15), calls=%async_computation | async-start | bytes 2097152 | tf_op jit(solution)/shard_map/all_to_all | solution.py:280
  19.8 0.7 copy-start.5
  19.9 0.7 copy-start.6
  27.6 27.8 %copy-start.7 = (f32[1024,128]{1,0:T(8,128)}, f32[1024,128]{1,0:T(8,128)S(1)}, u32[]{:S(2)}) copy-start(f32[1024,128]{1,0:T(8,128)S(1)} %get-tuple-element.24.bias_ref) | copy-start | bytes 1572868
  27.6 27.8 %copy-start.9 = (bf16[128,768]{1,0:T(8,128)(2,1)}, bf16[128,768]{1,0:T(8,128)(2,1)S(1)}, u32[]{:S(2)}) copy-start(bf16[128,768]{1,0:T(8,128)(2,1)S(1)} %get-tuple-element.23.d_att_t_hbm.d_att_t_ref) | copy-start | bytes 589828
  55.5 0.7 copy-start.11
  56.1 0.6 copy-start.13
  56.7 35.4 %all-to-all-start.1 = ((bf16[64,4,8,256]{3,2,1,0:T(8,128)(2,1)}), bf16[64,4,8,256]{3,2,1,0:T(8,128)(2,1)S(1)}, u32[]{:S(2)}, u32[]{:S(2)}) async-start(bf16[64,4,8,256]{3,2,1,0:T(8,128)(2,1)} %bitcast.5), calls=%async_computation.1 | async-start | bytes 2097152 | tf_op jit(solution)/shard_map/all_to_all | solution.py:280
  63.2 1.0 %copy-start.8 = (f32[1024,128]{1,0:T(8,128)S(1)}, f32[1024,128]{1,0:T(8,128)}, u32[]{:S(2)}) copy-start(f32[1024,128]{1,0:T(8,128)} %copy-done.7) | copy-start | bytes 1572868
  64.3 0.9 copy-start.10
  65.2 0.9 copy-start.12
  66.1 0.7 copy-start.14

commit v3 on v2

v3 whole, which is shorter than its diff:
```python
import math

import jax
import jax.numpy as jnp
from jax import lax
from jax.experimental import pallas as pl
from jax.experimental.pallas import tpu as pltpu
from jax.sharding import PartitionSpec as P

HD = 128
TILE = 8
SECTIONS = 4
ROWS = 128
PEERS = 64
GROUP = 6
SLOTS = PEERS * SECTIONS
KEYS = SLOTS * TILE
PICKS = 32
KEPT = SECTIONS * PICKS
NEAR = KEPT * TILE
WIDE = GROUP * ROWS
CHUNK = 256
PART = 256
N_CHUNK = NEAR // CHUNK
N_PART = WIDE // PART
SEND_PARTS = 4
FACTOR = 1.0 / math.sqrt(HD)
SCALE = FACTOR * math.log2(math.e)
HIDDEN = -1e30
INTERPRET = False
OWNER_LIMIT = 8 * 2**20
MAIN_LIMIT = 16 * 2**20

f32 = jnp.float32
bf16 = jnp.bfloat16


def dot(a, b):
    return lax.dot_general(a, b, (((1,), (0,)), ((), ())), preferred_element_type=f32)


def head(h):
    return slice(h * HD, (h + 1) * HD)


def owner_tiles(plan_ref, slot_ref, device):
    for b in range(PEERS):
        slot_ref[b * SECTIONS : (b + 1) * SECTIONS, :] = plan_ref[b].astype(f32)
    pick = (lax.broadcasted_iota(jnp.int32, (PEERS, HD), 0) == device).astype(bf16)
    return dot(slot_ref[...].astype(bf16), pick)


def owner_matrix(tiles):
    column = lax.broadcasted_iota(jnp.int32, (TILE, HD), 1)
    row = lax.broadcasted_iota(jnp.int32, (TILE, HD), 0)
    wanted = jnp.where((column & (TILE - 1)) == row, (column >> 3).astype(f32), -2.0)
    slots = tiles.shape[0]
    wide = jnp.broadcast_to(tiles[:, None, :], (slots, TILE, HD))
    return jnp.where(wide == wanted[None], 1.0, 0.0).reshape(slots * TILE, HD).astype(bf16)


def send_kernel(plan_hbm, key_hbm, value_hbm, out_hbm, plan_ref, key_ref, value_ref, out_ref, slot_ref, sems):
    loads = [
        pltpu.make_async_copy(plan_hbm, plan_ref, sems.at[0]),
        pltpu.make_async_copy(key_hbm, key_ref, sems.at[1]),
        pltpu.make_async_copy(value_hbm, value_ref, sems.at[2]),
    ]
    for load in loads:
        load.start()
    for load in loads:
        load.wait()
    tiles = owner_tiles(plan_ref, slot_ref, lax.axis_index("ctx"))
    both = jnp.concatenate([key_ref[...], value_ref[...]], axis=1)
    stores = []
    for c in range(SEND_PARTS):
        size = KEYS // SEND_PARTS
        matrix = owner_matrix(tiles[c * size // TILE : (c + 1) * size // TILE])
        out_ref[c * size : (c + 1) * size, :] = dot(matrix, both).astype(bf16)
        part = pl.ds(c * size, size)
        stores.append(pltpu.make_async_copy(out_ref.at[part], out_hbm.at[part], sems.at[3 + c]))
        stores[-1].start()
    for store in stores:
        store.wait()


def row_gate(logit_ref):
    return jax.nn.sigmoid(logit_ref[...])


def causal_scores(key_ref, query_t):
    scores = dot(key_ref[...], query_t)
    key_at = lax.broadcasted_iota(jnp.int32, (ROWS, WIDE), 0)
    row_at = lax.broadcasted_iota(jnp.int32, (ROWS, WIDE), 1) & (ROWS - 1)
    return jnp.where(row_at >= key_at, scores, HIDDEN)


def local_kernel(
    plan_ref, kind_ref, query_ref, key_ref, value_ref, grad_ref, logit_ref,
    query_t_ref, query_s_ref, d_att_t_ref, flag_ref, start_ref, out_t_ref, list_ref,
):
    gate = row_gate(logit_ref)
    for h in range(GROUP):
        block = query_ref[:, head(h)]
        query_s_ref[head(h), :] = block
        query_t_ref[:HD, head(h)] = block.astype(f32).T.astype(bf16)
        grad_t = grad_ref[:, head(h)].astype(f32).T
        d_att_t_ref[:, head(h)] = (gate * grad_t).astype(bf16)
    scores = causal_scores(key_ref, query_t_ref[:HD, :])
    top = jnp.max(scores, axis=0, keepdims=True)
    weights = jnp.exp2((scores - top) * SCALE)
    start_ref[0:1, :] = top
    start_ref[1:2, :] = jnp.sum(weights, axis=0, keepdims=True)
    value_t = value_ref[...].astype(f32).T.astype(bf16)
    out_t_ref[...] = dot(value_t, weights.astype(bf16))
    device = lax.axis_index("ctx")
    flag = lax.broadcasted_iota(jnp.int32, (HD, WIDE), 0)
    early = (lax.broadcasted_iota(jnp.int32, (HD, WIDE), 1) & (ROWS - 1)) < ROWS // 2
    query_t_ref[HD:, :] = jnp.where((flag == 0) | ((flag == 1) & early), HIDDEN, 0.0).astype(bf16)
    lane = lax.broadcasted_iota(jnp.int32, (TILE, HD), 1)
    flag_ref[...] = (lax.broadcasted_iota(jnp.int32, (NEAR, HD), 1) == 0).astype(bf16)
    for s in range(SECTIONS):

        @pl.loop(0, PICKS)
        def _(k):
            list_ref[s * PICKS + k] = device * SECTIONS + s

        def place(p, count):
            given = plan_ref[s, p] >= 0

            @pl.when(given)
            def _():
                list_ref[s * PICKS + count] = p * SECTIONS + s
                at = pl.multiple_of((s * PICKS + count) * TILE, TILE)
                chosen = jnp.where(kind_ref[s, p] == 0, -1, 1)
                flag_ref[pl.ds(at, TILE), :] = (lane == chosen).astype(bf16)

            return count + given.astype(jnp.int32)

        lax.fori_loop(0, PEERS, place, jnp.int32(0))


def main_kernel(
    slots_ref, list_hbm, query_t_hbm, flag_hbm, start_hbm, query_s_hbm, d_att_t_hbm, out_t_hbm,
    grad_hbm, att_t_hbm, stat_hbm, kv_hbm,
    list_ref, query_t_ref, flag_ref, start_ref, query_s_ref, d_att_t_ref, out_t_ref,
    grad_ref, att_t_ref, stat_ref, kv_ref, score_ref, weight_ref, d_score_ref, d_low_ref, sems,
):
    sources = (list_hbm, query_t_hbm, flag_hbm, start_hbm, query_s_hbm, d_att_t_hbm, out_t_hbm)
    places = (list_ref, query_t_ref, flag_ref, start_ref, query_s_ref, d_att_t_ref, out_t_ref)
    loads = [
        pltpu.make_async_copy(source, place, sems.at[n])
        for n, (source, place) in enumerate(zip(sources, places, strict=True))
    ]
    for load in loads:
        load.start()
    grad_ref[...] = jnp.zeros_like(grad_ref)
    for load in loads:
        load.wait()
    for k in range(KEPT):
        kv_ref[k * TILE : (k + 1) * TILE, :] = slots_ref[list_ref[k]]
    value_t = kv_ref[:, HD:].T
    chunks = [slice(c * CHUNK, (c + 1) * CHUNK) for c in range(N_CHUNK)]
    parts = [slice(n * PART, (n + 1) * PART) for n in range(N_PART)]
    tops, totals, outs, deltas, lows = [], [], [], [], []

    def score(n):
        top = jnp.broadcast_to(start_ref[0:1, parts[n]], (TILE, PART))
        for rows in chunks:
            keys = jnp.concatenate([kv_ref[rows, :HD], flag_ref[rows, :]], axis=1)
            scores = dot(keys, query_t_ref[:, parts[n]])
            score_ref[rows, parts[n]] = scores
            top = jnp.maximum(top, jnp.max(scores.reshape(CHUNK // TILE, TILE, PART), axis=0))
        tops.append(jnp.max(top, axis=0, keepdims=True))

    def weigh(n):
        total = jnp.zeros((TILE, PART), f32)
        for rows in chunks:
            weights = jnp.exp2((score_ref[rows, parts[n]] - tops[n]) * SCALE)
            total = total + jnp.sum(weights.reshape(CHUNK // TILE, TILE, PART), axis=0)
            weight_ref[rows, parts[n]] = weights.astype(bf16)
        totals.append(jnp.sum(total, axis=0, keepdims=True))
        outs.append(dot(value_t, weight_ref[:, parts[n]]))

    def finish(n):
        share = jnp.exp2((start_ref[0:1, parts[n]] - tops[n]) * SCALE)
        inverse = 1.0 / (totals[n] + share * start_ref[1:2, parts[n]])
        att_t = ((outs[n] + share * out_t_ref[:, parts[n]]) * inverse).astype(bf16)
        att_t_ref[:, parts[n]] = att_t
        d_att_t = d_att_t_ref[:, parts[n]].astype(f32)
        deltas.append(jnp.sum(d_att_t * att_t.astype(f32), axis=0, keepdims=True) * inverse)
        lows.append((d_att_t * inverse).astype(bf16))
        for h in range(PART // HD):
            at = n * PART + h * HD
            d_low_ref[at : at + HD, :] = lows[n][:, head(h)].T
        stat_ref[0:1, parts[n]] = tops[n]
        stat_ref[1:2, parts[n]] = inverse
        stat_ref[2:3, parts[n]] = deltas[n]

    def back(n):
        for rows in chunks:
            d_probs = dot(kv_ref[rows, HD:], lows[n])
            weights = weight_ref[rows, parts[n]].astype(f32)
            d_score_ref[rows, parts[n]] = (weights * (d_probs - deltas[n])).astype(bf16)

    score(0)
    for n in range(N_PART):
        if n + 1 < N_PART:
            score(n + 1)
        weigh(n)
        if n > 0:
            back(n - 1)
        finish(n)
    back(N_PART - 1)
    stores = [
        pltpu.make_async_copy(att_t_ref, att_t_hbm, sems.at[8]),
        pltpu.make_async_copy(stat_ref, stat_hbm, sems.at[9]),
        pltpu.make_async_copy(kv_ref, kv_hbm, sems.at[7]),
    ]

    def scatter(values, c, side):
        for k in range(CHUNK // TILE):
            slot = list_ref[c * (CHUNK // TILE) + k]
            grad_ref[slot, :, side * HD : (side + 1) * HD] = values[k * TILE : (k + 1) * TILE, :]

    def send(side):
        half = pl.ds(side * HD, HD)
        stores.append(
            pltpu.make_async_copy(grad_ref.at[:, :, half], grad_hbm.at[:, :, half], sems.at[10 + side])
        )
        stores[-1].start()

    for store in stores:
        store.start()
    for c in range(N_CHUNK):
        scatter(dot(weight_ref[chunks[c], :], d_low_ref[...]).astype(bf16), c, 1)
    send(1)
    for c in range(N_CHUNK):
        scatter((dot(d_score_ref[chunks[c], :], query_s_ref[...]) * FACTOR).astype(bf16), c, 0)
    send(0)
    for store in stores:
        store.wait()


def query_kernel(
    plan_ref, kv_ref, key_ref, value_ref, grad_ref, query_t_ref, query_s_ref, d_att_t_ref, flag_ref,
    att_t_ref, stat_ref, query_grad_ref, local_ref, gate_ref, owner_ref, slot_ref,
):
    top, inverse, delta = stat_ref[0:1, :], stat_ref[1:2, :], stat_ref[2:3, :]
    d_low_t = (d_att_t_ref[...].astype(f32) * inverse).astype(bf16)
    d_low_s = jnp.concatenate([d_low_t[:, head(h)].T for h in range(GROUP)], axis=0)

    def d_score(scores, values):
        weights = jnp.exp2((scores - top) * SCALE)
        d_scores = (weights * (dot(values, d_low_t) - delta)).astype(bf16)
        return weights.astype(bf16), d_scores

    weights, d_scores = d_score(causal_scores(key_ref, query_t_ref[:HD, :]), value_ref[...])
    local_ref[:, :HD] = dot(d_scores, query_s_ref[...]) * FACTOR
    local_ref[:, HD:] = dot(weights, d_low_s)
    total = dot(key_ref[...].T, d_scores)
    for c in range(N_CHUNK):
        rows = slice(c * CHUNK, (c + 1) * CHUNK)
        keys = kv_ref[rows, :HD]
        scores = dot(jnp.concatenate([keys, flag_ref[rows, :]], axis=1), query_t_ref[...])
        _, d_scores = d_score(scores, kv_ref[rows, HD:])
        total = total + dot(keys.T, d_scores)
    part = jnp.zeros((1, ROWS), f32)
    for h in range(GROUP):
        query_grad_ref[:, head(h)] = (total[:, head(h)] * FACTOR).T.astype(bf16)
        grad_t = grad_ref[:, head(h)].astype(f32).T
        part = part + jnp.sum(grad_t * att_t_ref[:, head(h)].astype(f32), axis=0, keepdims=True)
    gate_ref[...] = part
    matrix = owner_matrix(owner_tiles(plan_ref, slot_ref, lax.axis_index("ctx")))
    for c in range(KEYS // HD):
        owner_ref[:, c * HD : (c + 1) * HD] = matrix[c * HD : (c + 1) * HD, :].T


def owner_kernel(owner_ref, returned_ref, local_ref, key_grad_ref, value_grad_ref):
    total = local_ref[...] + dot(owner_ref[...], returned_ref[...])
    key_grad_ref[...] = total[:, :HD].astype(bf16)
    value_grad_ref[...] = total[:, HD:].astype(bf16)


VMEM = pltpu.VMEM
SMEM = pltpu.SMEM
HBM = pltpu.HBM


def call(kernel, ins, outs, scratch, flops, moved, limit=None):
    return pl.pallas_call(
        kernel,
        out_shape=[HBM(shape, kind) if space is HBM else jax.ShapeDtypeStruct(shape, kind) for space, shape, kind in outs],
        in_specs=[pl.BlockSpec(memory_space=space) for space, _ in ins],
        out_specs=[pl.BlockSpec(memory_space=space) for space, _, _ in outs],
        scratch_shapes=scratch,
        compiler_params=pltpu.CompilerParams(vmem_limit_bytes=limit),
        cost_estimate=pl.CostEstimate(flops=flops, bytes_accessed=moved, transcendentals=0),
        interpret=INTERPRET,
        name=kernel.__name__,
    )(*[pltpu.with_memory_space_constraint(array, HBM) if space is HBM else array for space, array in ins])


def exchange(pieces):
    return lax.all_to_all(pieces, "ctx", split_axis=0, concat_axis=0, tiled=True)


def body(queries, key_rows, value_rows, out_grad, gate_logit, tile_plan, mask_kind):
    logit = gate_logit.reshape(1, ROWS)
    plan_row = lax.dynamic_index_in_dim(tile_plan, lax.axis_index("ctx"), 0, keepdims=False)
    (outgoing,) = call(
        send_kernel,
        [(HBM, tile_plan), (HBM, key_rows), (HBM, value_rows)],
        [(HBM, (KEYS, 2 * HD), bf16)],
        [VMEM((PEERS, SECTIONS, PEERS), jnp.int32), VMEM((ROWS, HD), bf16), VMEM((ROWS, HD), bf16),
         VMEM((KEYS, 2 * HD), bf16),
         VMEM((SLOTS, PEERS), f32), pltpu.SemaphoreType.DMA((3 + SEND_PARTS,))],
        2**27, 2**21,
    )
    fetched = exchange(outgoing.reshape(PEERS, SECTIONS, TILE, 2 * HD)).reshape(SLOTS, TILE, 2 * HD)
    query_t, query_s, d_att_t, flags, start, out_t, places = call(
        local_kernel,
        [(SMEM, plan_row), (SMEM, mask_kind[0]), (VMEM, queries), (VMEM, key_rows), (VMEM, value_rows),
         (VMEM, out_grad), (VMEM, logit)],
        [(VMEM, (2 * HD, WIDE), bf16), (VMEM, (WIDE, HD), bf16), (VMEM, (HD, WIDE), bf16), (VMEM, (NEAR, HD), bf16),
         (VMEM, (8, WIDE), f32), (VMEM, (HD, WIDE), f32), (SMEM, (KEPT,), jnp.int32)],
        [], 2**27, 2**22,
    )
    grads, att_t, stat, near = call(
        main_kernel,
        [(VMEM, fetched), (HBM, places), (HBM, query_t), (HBM, flags), (HBM, start), (HBM, query_s), (HBM, d_att_t),
         (HBM, out_t)],
        [(HBM, (SLOTS, TILE, 2 * HD), bf16), (HBM, (HD, WIDE), bf16), (HBM, (8, WIDE), f32), (HBM, (NEAR, 2 * HD), bf16)],
        [SMEM((KEPT,), jnp.int32), VMEM((2 * HD, WIDE), bf16), VMEM((NEAR, HD), bf16),
         VMEM((8, WIDE), f32), VMEM((WIDE, HD), bf16), VMEM((HD, WIDE), bf16), VMEM((HD, WIDE), f32),
         VMEM((SLOTS, TILE, 2 * HD), bf16), VMEM((HD, WIDE), bf16), VMEM((8, WIDE), f32), VMEM((NEAR, 2 * HD), bf16),
         VMEM((NEAR, WIDE), f32), VMEM((NEAR, WIDE), bf16), VMEM((NEAR, WIDE), bf16), VMEM((WIDE, HD), bf16),
         pltpu.SemaphoreType.DMA((12,))],
        2**30, 2**22, limit=MAIN_LIMIT,
    )
    returned = exchange(grads.reshape(PEERS, SECTIONS, TILE, 2 * HD)).reshape(KEYS, 2 * HD)
    query_grad, local, gate_part, owner = call(
        query_kernel,
        [(VMEM, tile_plan), (VMEM, near), (VMEM, key_rows), (VMEM, value_rows), (VMEM, out_grad),
         (VMEM, query_t), (VMEM, query_s), (VMEM, d_att_t), (VMEM, flags), (VMEM, att_t), (VMEM, stat)],
        [(VMEM, (ROWS, WIDE), bf16), (VMEM, (ROWS, 2 * HD), f32), (VMEM, (1, ROWS), f32), (VMEM, (HD, KEYS), bf16)],
        [VMEM((SLOTS, PEERS), f32)],
        2**30, 2**22,
    )
    gate = jax.nn.sigmoid(gate_logit)
    gate_sum = lax.all_gather(gate_part[0], "head").sum(0)
    gate_grad = gate * (1.0 - gate) * gate_sum
    key_grad, value_grad = call(
        owner_kernel,
        [(VMEM, owner), (VMEM, returned), (VMEM, local)],
        [(VMEM, (ROWS, HD), bf16), (VMEM, (ROWS, HD), bf16)],
        [], 2**27, 2**21, limit=OWNER_LIMIT,
    )
    return (query_grad, key_grad, value_grad, gate_grad)


def solution(mesh):
    placed = (
        P("ctx", "head"),
        P("ctx", "head"),
        P("ctx", "head"),
        P("ctx", "head"),
        P("ctx"),
        P(),
        P("ctx", None, None),
    )
    return jax.shard_map(
        body,
        mesh=mesh,
        in_specs=placed,
        out_specs=(P("ctx", "head"), P("ctx", "head"), P("ctx", "head"), P("ctx")),
        check_vma=False,
    )
```

time: 93.6 us -> 93.2 us (level)
  Pallas kernels: 19.6 us -> 21.2 us
  local copies, waits for them, and re-layouts: 5.58 us -> 4.49 us
    unnamed x30 -> x8, local copies, waits for them, and re-layouts: 5.57 us -> 3.23 us
    pallas_call x5, Pallas kernels: 19.6 us -> 21.2 us  [call(): pl.pallas_call(kernel, out_shape=[HBM(shape, kind) if space is HBM else j...]
    squeeze x1, local copies, waits for them, and re-layouts: 0.01 us -> 1.26 us  [body(): lax.dynamic_index_in_dim(tile_plan, lax.axis_index('ctx'), 0, keepdims=Fa...]
  transfers between devices with their start and end apart: 2 -> 2, of which waited for: 2 -> 2; matrix products, arithmetic and copies ran while one was open for 1% -> 2% of each run, Pallas kernels for 11% -> 14%
where the time goes in v3:
time: 93.2 us; the launch traced here: 92.7 us
  waiting for transfers between devices  35.3 us (38%)
  starting transfers between devices  23.1 us (25%)
  Pallas kernels  21.2 us (23%)
  blocking collectives  7.39 us (8%)
  local copies, waits for them, and re-layouts  4.49 us (5%)
    all_to_all x2, waiting for transfers between devices, exchange(): lax.all_to_all(pieces, 'ctx', split_axis=0, concat_axis=0, tiled=True)  35.3 us
    all_to_all x2, starting transfers between devices, exchange(): lax.all_to_all(pieces, 'ctx', split_axis=0, concat_axis=0, tiled=True)  23.1 us
    pallas_call x5, Pallas kernels, call(): pl.pallas_call(kernel, out_shape=[HBM(shape, kind) if space is HBM else j...  21.2 us
    all_gather x1, blocking collectives, body(): gate_sum = lax.all_gather(gate_part[0], 'head').sum(0)  7.39 us
    unnamed x8, local copies, waits for them, and re-layouts  3.23 us
  transfers between devices with their start and end apart: 2, of which 2 were waited for; matrix products, arithmetic and copies ran while one was open for 2% of the time, Pallas kernels for 14%

profile of v3, /device:TPU:6, one launch (start us, length us, event | category | flops | bytes accessed | tf_op | source)
XLA Modules:
  0.0 92.7 jit_solution(13234740812756416294)
XLA Ops:
  0.6 2.3 %send_kernel.1 = bf16[2048,256]{1,0:T(8,128)(2,1)} custom-call(s32[64,4,64]{2,1,0:T(4,128)} %plan_ref.1, bf16[128,128]{1,0:T(8,128)(2,1)} %key_ref.3, bf16[128,128]{1,0:T(8,128)(2,1)} %value_ref.3), custom_call_target="tpu_custom_call" | custom-call | flops 134217728 | bytes 2097152 | tf_op jit(solution)/shard_map/send_kernel/pallas_call | solution.py:290
  3.0 16.6 %all-to-all-start = ((bf16[64,4,8,256]{3,2,1,0:T(8,128)(2,1)}), bf16[64,4,8,256]{3,2,1,0:T(8,128)(2,1)S(1)}, u32[]{:S(2)}, u32[]{:S(2)}) async-start(bf16[64,4,8,256]{3,2,1,0:T(8,128)(2,1)} %bitcast.11), calls=%async_computation | async-start | bytes 2097152 | tf_op jit(solution)/shard_map/all_to_all | solution.py:304
  19.6 1.3 %dynamic-slice_bitcast_fusion.plan_ref = s32[4,64]{1,0:T(4,128)} fusion(s32[64,4,64]{2,1,0:T(4,128)} %plan_ref.1, s32[]{:T(128)S(6)} %select_n.4), kind=kLoop, calls=%fused_computation | loop fusion | bytes 2052 | tf_op jit(solution)/shard_map/jit(dynamic_index_in_dim)/squeeze | solution.py:309
  20.9 8.2 %local_kernel.1 = (bf16[256,768]{1,0:T(8,128)(2,1)}, bf16[768,128]{1,0:T(8,128)(2,1)}, bf16[128,768]{1,0:T(8,128)(2,1)}, bf16[1024,128]{1,0:T(8,128)(2,1)}, f32[...) custom-call(s32[4,64]{1,0:T(4,128)} %dynamic-slice_bitcast_fusion.plan_ref, s32[4,64]{1,0:T(4,128)} %bitcast.14, ...), custom_call_target="tpu_custom_call" | custom-call | flops 134217728 | bytes 4194304 | tf_op jit(solution)/shard_map/local_kernel/pallas_call | solution.py:290
  29.0 20.3 %all-to-all-done = bf16[64,4,8,256]{3,2,1,0:T(8,128)(2,1)S(1)} async-done(((bf16[64,4,8,256]{3,2,1,0:T(8,128)(2,1)}), bf16[64,4,8,256]{3,2,1,0:T(8,128)(2,1)S(1)}, u32[]{:S(2)}, u32[]{:S(2)}) %all-to-all-start) | async-done | bytes 1048608 | tf_op jit(solution)/shard_map/all_to_all | solution.py:304
  49.4 5.1 %main_kernel.1 = (bf16[256,8,256]{2,1,0:T(8,128)(2,1)}, bf16[128,768]{1,0:T(8,128)(2,1)}, f32[8,768]{1,0:T(8,128)}, bf16[1024,256]{1,0:T(8,128)(2,1)}) custom-call(bf16[256,8,256]{2,1,0:T(8,128)(2,1)S(1)} %bitcast.10, s32[128]{0:T(128)} %get-tuple-element.21.list_hbm, bf16[256,768]{1,0:T(8,128)(2,1)} %get-tuple-element.22.query_t_hbm.query_t_ref, ...), custom_call_target="tpu_custom_call" | custom-call | flops 1073741824 | bytes 4194304 | tf_op jit(solution)/shard_map/main_kernel/pallas_call | solution.py:290
  54.5 6.5 %all-to-all-start.1 = ((bf16[64,4,8,256]{3,2,1,0:T(8,128)(2,1)}), bf16[64,4,8,256]{3,2,1,0:T(8,128)(2,1)S(1)}, u32[]{:S(2)}, u32[]{:S(2)}) async-start(bf16[64,4,8,256]{3,2,1,0:T(8,128)(2,1)} %bitcast.12), calls=%async_computation.1 | async-start | bytes 2097152 | tf_op jit(solution)/shard_map/all_to_all | solution.py:304
  61.0 4.6 %query_kernel.1 = (bf16[128,768]{1,0:T(8,128)(2,1)}, f32[128,256]{1,0:T(8,128)}, f32[1,128]{1,0:T(1,128)}, bf16[128,2048]{1,0:T(8,128)(2,1)}) custom-call(s32[64,4,64]{2,1,0:T(4,128)} %plan_ref.1, bf16[1024,256]{1,0:T(8,128)(2,1)} %get-tuple-element.28.kv_ref, bf16[128,128]{1,0:T(8,128)(2,1)} %key_ref.3, bf16[128,128]{1,0:T(8,128)(2,1)} %value_ref.3, ...), custom_call_target="tpu_custom_call" | custom-call | flops 1073741824 | bytes 4194304 | tf_op jit(solution)/shard_map/query_kernel/pallas_call | solution.py:290
  65.6 0.0 copy-start.2
  65.6 0.7 copy-done.2
  66.3 7.4 %all-gather = f32[8,1,128]{2,1,0:T(1,128)S(1)} all-gather(f32[1,1,128]{2,1,0:T(1,128)S(1)} %bitcast.13), channel_id=1, replica_groups=mesh['head'=8,'ctx'=64] {'head'}, dimensions={0}, use_global_device_ids=true | all-gather | bytes 4608 | tf_op jit(solution)/shard_map/all_gather | solution.py:350
  73.7 0.0 copy-start.3
  73.7 0.6 copy-done.3
  74.3 0.5 fusion
  74.8 15.0 %all-to-all-done.1 = bf16[64,4,8,256]{3,2,1,0:T(8,128)(2,1)S(1)} async-done(((bf16[64,4,8,256]{3,2,1,0:T(8,128)(2,1)}), bf16[64,4,8,256]{3,2,1,0:T(8,128)(2,1)S(1)}, u32[]{:S(2)}, u32[]{:S(2)}) %all-to-all-start.1) | async-done | bytes 1048608 | tf_op jit(solution)/shard_map/all_to_all | solution.py:304
  89.8 0.0 copy-start
  89.9 1.0 %copy-done = bf16[128,2048]{1,0:T(8,128)(2,1)S(1)} copy-done((bf16[128,2048]{1,0:T(8,128)(2,1)S(1)}, bf16[128,2048]{1,0:T(8,128)(2,1)}, u32[]{:S(2)}) %copy-start) | copy-done | bytes 524312
  90.9 0.0 copy-start.1
  90.9 0.9 copy-done.1
  91.8 0.9 %owner_kernel.1 = (bf16[128,128]{1,0:T(8,128)(2,1)}, bf16[128,128]{1,0:T(8,128)(2,1)}) custom-call(bf16[128,2048]{1,0:T(8,128)(2,1)S(1)} %copy-done, bf16[2048,256]{1,0:T(8,128)(2,1)S(1)} %bitcast.9, f32[128,256]{1,0:T(8,128)S(1)} %copy-done.1), custom_call_target="tpu_custom_call" | custom-call | flops 134217728 | bytes 2097152 | tf_op jit(solution)/shard_map/owner_kernel/pallas_call | solution.py:290
  (1 shorter events, 0.0 us)
Async XLA Ops:
  3.0 46.4 %all-to-all-start = ((bf16[64,4,8,256]{3,2,1,0:T(8,128)(2,1)}), bf16[64,4,8,256]{3,2,1,0:T(8,128)(2,1)S(1)}, u32[]{:S(2)}, u32[]{:S(2)}) async-start(bf16[64,4,8,256]{3,2,1,0:T(8,128)(2,1)} %bitcast.11), calls=%async_computation | async-start | bytes 2097152 | tf_op jit(solution)/shard_map/all_to_all | solution.py:304
  54.5 35.4 %all-to-all-start.1 = ((bf16[64,4,8,256]{3,2,1,0:T(8,128)(2,1)}), bf16[64,4,8,256]{3,2,1,0:T(8,128)(2,1)S(1)}, u32[]{:S(2)}, u32[]{:S(2)}) async-start(bf16[64,4,8,256]{3,2,1,0:T(8,128)(2,1)} %bitcast.12), calls=%async_computation.1 | async-start | bytes 2097152 | tf_op jit(solution)/shard_map/all_to_all | solution.py:304
  65.6 0.7 copy-start.2
  73.7 0.7 copy-start.3
  89.8 1.0 %copy-start = (bf16[128,2048]{1,0:T(8,128)(2,1)S(1)}, bf16[128,2048]{1,0:T(8,128)(2,1)}, u32[]{:S(2)}) copy-start(bf16[128,2048]{1,0:T(8,128)(2,1)} %get-tuple-element.32.owner_ref) | copy-start | bytes 1572868
  90.9 0.9 copy-start.1

commit v4 on v3

--- a/solution.py
+++ b/solution.py
@@ -28,8 +28,7 @@
 SCALE = FACTOR * math.log2(math.e)
 HIDDEN = -1e30
 INTERPRET = False
-OWNER_LIMIT = 8 * 2**20
-MAIN_LIMIT = 16 * 2**20
+VMEM_LIMIT = 16 * 2**20
 
 f32 = jnp.float32
 bf16 = jnp.bfloat16
@@ -97,6 +96,7 @@
 def local_kernel(
     plan_ref, kind_ref, query_ref, key_ref, value_ref, grad_ref, logit_ref,
     query_t_ref, query_s_ref, d_att_t_ref, flag_ref, start_ref, out_t_ref, list_ref,
+    query_t_hbm, query_s_hbm, d_att_t_hbm, flag_hbm, sems,
 ):
     gate = row_gate(logit_ref)
     for h in range(GROUP):
@@ -137,25 +137,24 @@
             return count + given.astype(jnp.int32)
 
         lax.fori_loop(0, PEERS, place, jnp.int32(0))
+    sources = (query_t_ref, query_s_ref, d_att_t_ref, flag_ref)
+    copies = (query_t_hbm, query_s_hbm, d_att_t_hbm, flag_hbm)
+    stores = [
+        pltpu.make_async_copy(source, copy, sems.at[n])
+        for n, (source, copy) in enumerate(zip(sources, copies, strict=True))
+    ]
+    for store in stores:
+        store.start()
+    for store in stores:
+        store.wait()
 
 
 def main_kernel(
-    slots_ref, list_hbm, query_t_hbm, flag_hbm, start_hbm, query_s_hbm, d_att_t_hbm, out_t_hbm,
+    list_ref, slots_ref, query_t_ref, flag_ref, start_ref, query_s_ref, d_att_t_ref, out_t_ref,
     grad_hbm, att_t_hbm, stat_hbm, kv_hbm,
-    list_ref, query_t_ref, flag_ref, start_ref, query_s_ref, d_att_t_ref, out_t_ref,
     grad_ref, att_t_ref, stat_ref, kv_ref, score_ref, weight_ref, d_score_ref, d_low_ref, sems,
 ):
-    sources = (list_hbm, query_t_hbm, flag_hbm, start_hbm, query_s_hbm, d_att_t_hbm, out_t_hbm)
-    places = (list_ref, query_t_ref, flag_ref, start_ref, query_s_ref, d_att_t_ref, out_t_ref)
-    loads = [
-        pltpu.make_async_copy(source, place, sems.at[n])
-        for n, (source, place) in enumerate(zip(sources, places, strict=True))
-    ]
-    for load in loads:
-        load.start()
     grad_ref[...] = jnp.zeros_like(grad_ref)
-    for load in loads:
-        load.wait()
     for k in range(KEPT):
         kv_ref[k * TILE : (k + 1) * TILE, :] = slots_ref[list_ref[k]]
     value_t = kv_ref[:, HD:].T
@@ -212,9 +211,9 @@
         finish(n)
     back(N_PART - 1)
     stores = [
-        pltpu.make_async_copy(att_t_ref, att_t_hbm, sems.at[8]),
-        pltpu.make_async_copy(stat_ref, stat_hbm, sems.at[9]),
-        pltpu.make_async_copy(kv_ref, kv_hbm, sems.at[7]),
+        pltpu.make_async_copy(att_t_ref, att_t_hbm, sems.at[1]),
+        pltpu.make_async_copy(stat_ref, stat_hbm, sems.at[2]),
+        pltpu.make_async_copy(kv_ref, kv_hbm, sems.at[0]),
     ]
 
     def scatter(values, c, side):
@@ -225,7 +224,7 @@
     def send(side):
         half = pl.ds(side * HD, HD)
         stores.append(
-            pltpu.make_async_copy(grad_ref.at[:, :, half], grad_hbm.at[:, :, half], sems.at[10 + side])
+            pltpu.make_async_copy(grad_ref.at[:, :, half], grad_hbm.at[:, :, half], sems.at[3 + side])
         )
         stores[-1].start()
 
@@ -317,34 +316,33 @@
         2**27, 2**21,
     )
     fetched = exchange(outgoing.reshape(PEERS, SECTIONS, TILE, 2 * HD)).reshape(SLOTS, TILE, 2 * HD)
-    query_t, query_s, d_att_t, flags, start, out_t, places = call(
+    query_t, query_s, d_att_t, flags, start, out_t, places, *again = call(
         local_kernel,
         [(SMEM, plan_row), (SMEM, mask_kind[0]), (VMEM, queries), (VMEM, key_rows), (VMEM, value_rows),
          (VMEM, out_grad), (VMEM, logit)],
         [(VMEM, (2 * HD, WIDE), bf16), (VMEM, (WIDE, HD), bf16), (VMEM, (HD, WIDE), bf16), (VMEM, (NEAR, HD), bf16),
-         (VMEM, (8, WIDE), f32), (VMEM, (HD, WIDE), f32), (SMEM, (KEPT,), jnp.int32)],
-        [], 2**27, 2**22,
+         (VMEM, (8, WIDE), f32), (VMEM, (HD, WIDE), f32), (SMEM, (KEPT,), jnp.int32),
+         (HBM, (2 * HD, WIDE), bf16), (HBM, (WIDE, HD), bf16), (HBM, (HD, WIDE), bf16), (HBM, (NEAR, HD), bf16)],
+        [pltpu.SemaphoreType.DMA((4,))], 2**27, 2**22, limit=VMEM_LIMIT,
     )
     grads, att_t, stat, near = call(
         main_kernel,
-        [(VMEM, fetched), (HBM, places), (HBM, query_t), (HBM, flags), (HBM, start), (HBM, query_s), (HBM, d_att_t),
-         (HBM, out_t)],
+        [(SMEM, places), (VMEM, fetched), (VMEM, query_t), (VMEM, flags), (VMEM, start), (VMEM, query_s), (VMEM, d_att_t),
+         (VMEM, out_t)],
         [(HBM, (SLOTS, TILE, 2 * HD), bf16), (HBM, (HD, WIDE), bf16), (HBM, (8, WIDE), f32), (HBM, (NEAR, 2 * HD), bf16)],
-        [SMEM((KEPT,), jnp.int32), VMEM((2 * HD, WIDE), bf16), VMEM((NEAR, HD), bf16),
-         VMEM((8, WIDE), f32), VMEM((WIDE, HD), bf16), VMEM((HD, WIDE), bf16), VMEM((HD, WIDE), f32),
-         VMEM((SLOTS, TILE, 2 * HD), bf16), VMEM((HD, WIDE), bf16), VMEM((8, WIDE), f32), VMEM((NEAR, 2 * HD), bf16),
+        [VMEM((SLOTS, TILE, 2 * HD), bf16), VMEM((HD, WIDE), bf16), VMEM((8, WIDE), f32), VMEM((NEAR, 2 * HD), bf16),
          VMEM((NEAR, WIDE), f32), VMEM((NEAR, WIDE), bf16), VMEM((NEAR, WIDE), bf16), VMEM((WIDE, HD), bf16),
-         pltpu.SemaphoreType.DMA((12,))],
-        2**30, 2**22, limit=MAIN_LIMIT,
+         pltpu.SemaphoreType.DMA((5,))],
+        2**30, 2**22, limit=VMEM_LIMIT,
     )
     returned = exchange(grads.reshape(PEERS, SECTIONS, TILE, 2 * HD)).reshape(KEYS, 2 * HD)
     query_grad, local, gate_part, owner = call(
         query_kernel,
         [(VMEM, tile_plan), (VMEM, near), (VMEM, key_rows), (VMEM, value_rows), (VMEM, out_grad),
-         (VMEM, query_t), (VMEM, query_s), (VMEM, d_att_t), (VMEM, flags), (VMEM, att_t), (VMEM, stat)],
+         *[(VMEM, array) for array in again], (VMEM, att_t), (VMEM, stat)],
         [(VMEM, (ROWS, WIDE), bf16), (VMEM, (ROWS, 2 * HD), f32), (VMEM, (1, ROWS), f32), (VMEM, (HD, KEYS), bf16)],
         [VMEM((SLOTS, PEERS), f32)],
-        2**30, 2**22,
+        2**30, 2**22, limit=VMEM_LIMIT,
     )
     gate = jax.nn.sigmoid(gate_logit)
     gate_sum = lax.all_gather(gate_part[0], "head").sum(0)
@@ -353,7 +351,7 @@
         owner_kernel,
         [(VMEM, owner), (VMEM, returned), (VMEM, local)],
         [(VMEM, (ROWS, HD), bf16), (VMEM, (ROWS, HD), bf16)],
-        [], 2**27, 2**21, limit=OWNER_LIMIT,
+        [], 2**27, 2**21, limit=VMEM_LIMIT,
     )
     return (query_grad, key_grad, value_grad, gate_grad)
 

time: 93.2 us -> 90.9 us (0.975)
  local copies, waits for them, and re-layouts: 4.49 us -> 1.73 us
  Pallas kernels: 21.2 us -> 18.7 us
  waiting for transfers between devices: 35.3 us -> 37.8 us
    all_to_all x2, waiting for transfers between devices: 35.3 us -> 37.8 us  [exchange(): lax.all_to_all(pieces, 'ctx', split_axis=0, concat_axis=0, tiled=True)]
    pallas_call x5, Pallas kernels: 21.2 us -> 18.7 us  [call(): pl.pallas_call(kernel, out_shape=[HBM(shape, kind) if space is HBM else j...]
    unnamed x8 -> x28, local copies, waits for them, and re-layouts: 3.23 us -> 1.73 us
    squeeze x1, local copies, waits for them, and re-layouts: 1.26 us -> 0.01 us  [body(): lax.dynamic_index_in_dim(tile_plan, lax.axis_index('ctx'), 0, keepdims=Fa...]
  transfers between devices with their start and end apart: 2 -> 2, of which waited for: 2 -> 2; matrix products, arithmetic and copies ran while one was open for 2% -> 1% of each run, Pallas kernels for 14% -> 12%
where the time goes in v4:
time: 90.9 us; the launch traced here: 90.5 us
  waiting for transfers between devices  37.8 us (42%)
  starting transfers between devices  23.4 us (26%)
  Pallas kernels  18.7 us (21%)
  blocking collectives  7.38 us (8%)
  local copies, waits for them, and re-layouts  1.73 us (2%)
    all_to_all x2, waiting for transfers between devices, exchange(): lax.all_to_all(pieces, 'ctx', split_axis=0, concat_axis=0, tiled=True)  37.8 us
    all_to_all x2, starting transfers between devices, exchange(): lax.all_to_all(pieces, 'ctx', split_axis=0, concat_axis=0, tiled=True)  23.4 us
    pallas_call x5, Pallas kernels, call(): pl.pallas_call(kernel, out_shape=[HBM(shape, kind) if space is HBM else j...  18.7 us
    all_gather x1, blocking collectives, body(): gate_sum = lax.all_gather(gate_part[0], 'head').sum(0)  7.38 us
  transfers between devices with their start and end apart: 2, of which 2 were waited for; matrix products, arithmetic and copies ran while one was open for 1% of the time, Pallas kernels for 12%

profile of v4, /device:TPU:6, one launch (start us, length us, event | category | flops | bytes accessed | tf_op | source)
XLA Modules:
  0.0 90.5 jit_solution(13085743825411239131)
XLA Ops:
  0.6 2.4 %send_kernel.1 = bf16[2048,256]{1,0:T(8,128)(2,1)} custom-call(s32[64,4,64]{2,1,0:T(4,128)} %plan_ref.1, bf16[128,128]{1,0:T(8,128)(2,1)} %key_ref.3, bf16[128,128]{1,0:T(8,128)(2,1)} %value_ref.3), custom_call_target="tpu_custom_call" | custom-call | flops 134217728 | bytes 2097152 | tf_op jit(solution)/shard_map/send_kernel/pallas_call | solution.py:289
  3.0 0.0 copy-start
  3.0 0.0 copy-start.1
  3.0 0.0 copy-start.2
  3.0 0.0 copy-start.3
  3.0 0.0 copy-start.4
  3.1 16.7 %all-to-all-start = ((bf16[64,4,8,256]{3,2,1,0:T(8,128)(2,1)}), bf16[64,4,8,256]{3,2,1,0:T(8,128)(2,1)S(1)}, u32[]{:S(2)}, u32[]{:S(2)}) async-start(bf16[64,4,8,256]{3,2,1,0:T(8,128)(2,1)} %bitcast.14), calls=%async_computation | async-start | bytes 2097152 | tf_op jit(solution)/shard_map/all_to_all | solution.py:303
  19.8 0.0 copy-done
  19.8 0.0 copy-start.5
  19.8 0.0 copy-start.6
  19.9 0.0 copy-done.1
  19.9 0.0 copy-done.2
  19.9 0.0 copy-done.3
  19.9 0.0 copy-done.4
  19.9 0.6 copy-done.5
  20.5 0.0 copy-done.6
  20.5 8.2 %local_kernel.1 = (bf16[256,768]{1,0:T(8,128)(2,1)S(1)}, bf16[768,128]{1,0:T(8,128)(2,1)S(1)}, bf16[128,768]{1,0:T(8,128)(2,1)S(1)}, bf16[1024,128]{1,0:T(8,128)...) custom-call(s32[4,64]{1,0:T(4,128)S(1)} %dynamic-slice_bitcast_fusio, ...), custom_call_target="tpu_custom_call" | custom-call | flops 134217728 | bytes 4194304 | tf_op jit(solution)/shard_map/local_kernel/pallas_call | solution.py:289
  28.7 20.8 %all-to-all-done = bf16[64,4,8,256]{3,2,1,0:T(8,128)(2,1)S(1)} async-done(((bf16[64,4,8,256]{3,2,1,0:T(8,128)(2,1)}), bf16[64,4,8,256]{3,2,1,0:T(8,128)(2,1)S(1)}, u32[]{:S(2)}, u32[]{:S(2)}) %all-to-all-start) | async-done | bytes 1048608 | tf_op jit(solution)/shard_map/all_to_all | solution.py:303
  49.6 4.4 %main_kernel.1 = (bf16[256,8,256]{2,1,0:T(8,128)(2,1)}, bf16[128,768]{1,0:T(8,128)(2,1)}, f32[8,768]{1,0:T(8,128)}, bf16[1024,256]{1,0:T(8,128)(2,1)}) custom-call(s32[128]{0:T(128)S(1)} %get-tuple-element.25.list_ref, bf16[256,8,256]{2,1,0:T(8,128)(2,1)S(1)} %bitcast.10, bf16[256,768]{1,0:T(8,128)(2,1)S(1)} %get-tuple-element.26.query_t_ref, ...), custom_call_target="tpu_custom_call" | custom-call | flops 1073741824 | bytes 4194304 | tf_op jit(solution)/shard_map/main_kernel/pallas_call | solution.py:289
  54.0 0.0 copy-start.7
  54.0 0.0 copy-start.8
  54.0 0.0 copy-start.9
  54.0 0.0 copy-start.10
  54.0 0.0 copy-start.12
  54.0 0.0 copy-start.13
  54.0 6.6 %all-to-all-start.1 = ((bf16[64,4,8,256]{3,2,1,0:T(8,128)(2,1)}), bf16[64,4,8,256]{3,2,1,0:T(8,128)(2,1)S(1)}, u32[]{:S(2)}, u32[]{:S(2)}) async-start(bf16[64,4,8,256]{3,2,1,0:T(8,128)(2,1)} %bitcast.15), calls=%async_computation.1 | async-start | bytes 2097152 | tf_op jit(solution)/shard_map/all_to_all | solution.py:303
  60.7 0.0 copy-done.7
  60.7 0.0 copy-done.8
  60.7 0.0 copy-done.9
  60.7 0.0 copy-done.10
  60.7 0.0 copy-done.12
  60.7 0.0 copy-done.13
  60.7 0.0 copy-start.11
  60.8 1.0 %copy-done.11 = bf16[1024,256]{1,0:T(8,128)(2,1)S(1)} copy-done((bf16[1024,256]{1,0:T(8,128)(2,1)S(1)}, bf16[1024,256]{1,0:T(8,128)(2,1)}, u32[]{:S(2)}) %copy-start.11) | copy-done | bytes 524312
  61.8 2.8 %query_kernel.1 = (bf16[128,768]{1,0:T(8,128)(2,1)}, f32[128,256]{1,0:T(8,128)S(1)}, f32[1,128]{1,0:T(1,128)S(1)}, bf16[128,2048]{1,0:T(8,128)(2,1)S(1)}) custom-call(s32[64,4,64]{2,1,0:T(4,128)S(1)} %copy-done, bf16[1024,256]{1,0:T(8,128)(2,1)S(1)} %copy-done.11, bf16[128,128]{1,0:T(8,128)(2,1)S(1)} %copy-done.1, bf16[128,128]{1,0:T(8,128)(2,1)S(1)} %copy-done.2, ...), custom_call_target="tpu_custom_call" | custom-call | flops 1073741824 | bytes 4194304 | tf_op jit(solution)/shard_map/query_kernel/pallas_call | solution.py:289
  64.6 7.4 %all-gather = f32[8,1,128]{2,1,0:T(1,128)S(1)} all-gather(f32[1,1,128]{2,1,0:T(1,128)S(1)} %bitcast.11), channel_id=1, replica_groups=mesh['head'=8,'ctx'=64] {'head'}, dimensions={0}, use_global_device_ids=true | all-gather | bytes 4608 | tf_op jit(solution)/shard_map/all_gather | solution.py:348
  72.0 0.5 fusion
  72.5 17.0 %all-to-all-done.1 = bf16[64,4,8,256]{3,2,1,0:T(8,128)(2,1)S(1)} async-done(((bf16[64,4,8,256]{3,2,1,0:T(8,128)(2,1)}), bf16[64,4,8,256]{3,2,1,0:T(8,128)(2,1)S(1)}, u32[]{:S(2)}, u32[]{:S(2)}) %all-to-all-start.1) | async-done | bytes 1048608 | tf_op jit(solution)/shard_map/all_to_all | solution.py:303
  89.6 0.9 %owner_kernel.1 = (bf16[128,128]{1,0:T(8,128)(2,1)}, bf16[128,128]{1,0:T(8,128)(2,1)}) custom-call(bf16[128,2048]{1,0:T(8,128)(2,1)S(1)} %get-tuple-element.40.owner_ref, bf16[2048,256]{1,0:T(8,128)(2,1)S(1)} %bitcast.9, f32[128,256]{1,0:T(8,128)S(1)} %get-tuple-element.42.local_ref), custom_call_target="tpu_custom_call" | custom-call | flops 134217728 | bytes 2097152 | tf_op jit(solution)/shard_map/owner_kernel/pallas_call | solution.py:289
  (2 shorter events, 0.0 us)
Async XLA Ops:
  3.0 16.8 %copy-start = (s32[64,4,64]{2,1,0:T(4,128)S(1)}, s32[64,4,64]{2,1,0:T(4,128)}, u32[]{:S(2)}) copy-start(s32[64,4,64]{2,1,0:T(4,128)} %plan_ref.1) | copy-start | bytes 196612
  3.0 16.8 %copy-start.1 = (bf16[128,128]{1,0:T(8,128)(2,1)S(1)}, bf16[128,128]{1,0:T(8,128)(2,1)}, u32[]{:S(2)}) copy-start(bf16[128,128]{1,0:T(8,128)(2,1)} %key_ref.3) | copy-start | bytes 98308
  3.0 16.8 %copy-start.2 = (bf16[128,128]{1,0:T(8,128)(2,1)S(1)}, bf16[128,128]{1,0:T(8,128)(2,1)}, u32[]{:S(2)}) copy-start(bf16[128,128]{1,0:T(8,128)(2,1)} %value_ref.3) | copy-start | bytes 98308
  3.0 16.8 %copy-start.3 = (bf16[128,768]{1,0:T(8,128)(2,1)S(1)}, bf16[128,768]{1,0:T(8,128)(2,1)}, u32[]{:S(2)}) copy-start(bf16[128,768]{1,0:T(8,128)(2,1)} %query_ref.1) | copy-start | bytes 589828
  3.0 16.8 %copy-start.4 = (bf16[128,768]{1,0:T(8,128)(2,1)S(1)}, bf16[128,768]{1,0:T(8,128)(2,1)}, u32[]{:S(2)}) copy-start(bf16[128,768]{1,0:T(8,128)(2,1)} %grad_ref.3) | copy-start | bytes 589828
  3.1 46.5 %all-to-all-start = ((bf16[64,4,8,256]{3,2,1,0:T(8,128)(2,1)}), bf16[64,4,8,256]{3,2,1,0:T(8,128)(2,1)S(1)}, u32[]{:S(2)}, u32[]{:S(2)}) async-start(bf16[64,4,8,256]{3,2,1,0:T(8,128)(2,1)} %bitcast.14), calls=%async_computation | async-start | bytes 2097152 | tf_op jit(solution)/shard_map/all_to_all | solution.py:303
  19.8 0.7 copy-start.5
  19.8 0.7 copy-start.6
  54.0 6.7 %copy-start.7 = (bf16[256,768]{1,0:T(8,128)(2,1)S(1)}, bf16[256,768]{1,0:T(8,128)(2,1)}, u32[]{:S(2)}) copy-start(bf16[256,768]{1,0:T(8,128)(2,1)} %get-tuple-element.33.query_t_ref) | copy-start | bytes 1179652
  54.0 6.7 %copy-start.8 = (bf16[1024,128]{1,0:T(8,128)(2,1)S(1)}, bf16[1024,128]{1,0:T(8,128)(2,1)}, u32[]{:S(2)}) copy-start(bf16[1024,128]{1,0:T(8,128)(2,1)} %get-tuple-element.36.flag_ref) | copy-start | bytes 786436
  54.0 6.7 %copy-start.9 = (bf16[768,128]{1,0:T(8,128)(2,1)S(1)}, bf16[768,128]{1,0:T(8,128)(2,1)}, u32[]{:S(2)}) copy-start(bf16[768,128]{1,0:T(8,128)(2,1)} %get-tuple-element.34.query_s_ref) | copy-start | bytes 589828
  54.0 6.7 %copy-start.10 = (bf16[128,768]{1,0:T(8,128)(2,1)S(1)}, bf16[128,768]{1,0:T(8,128)(2,1)}, u32[]{:S(2)}) copy-start(bf16[128,768]{1,0:T(8,128)(2,1)} %get-tuple-element.35.d_att_t_ref) | copy-start | bytes 589828
  54.0 6.7 %copy-start.12 = (bf16[128,768]{1,0:T(8,128)(2,1)S(1)}, bf16[128,768]{1,0:T(8,128)(2,1)}, u32[]{:S(2)}) copy-start(bf16[128,768]{1,0:T(8,128)(2,1)} %get-tuple-element.37.att_t_ref) | copy-start | bytes 589828
  54.0 6.7 %copy-start.13 = (f32[8,768]{1,0:T(8,128)S(1)}, f32[8,768]{1,0:T(8,128)}, u32[]{:S(2)}) copy-start(f32[8,768]{1,0:T(8,128)} %get-tuple-element.38.stat_ref) | copy-start | bytes 73732
  54.0 35.5 %all-to-all-start.1 = ((bf16[64,4,8,256]{3,2,1,0:T(8,128)(2,1)}), bf16[64,4,8,256]{3,2,1,0:T(8,128)(2,1)S(1)}, u32[]{:S(2)}, u32[]{:S(2)}) async-start(bf16[64,4,8,256]{3,2,1,0:T(8,128)(2,1)} %bitcast.15), calls=%async_computation.1 | async-start | bytes 2097152 | tf_op jit(solution)/shard_map/all_to_all | solution.py:303
  60.7 1.0 %copy-start.11 = (bf16[1024,256]{1,0:T(8,128)(2,1)S(1)}, bf16[1024,256]{1,0:T(8,128)(2,1)}, u32[]{:S(2)}) copy-start(bf16[1024,256]{1,0:T(8,128)(2,1)} %get-tuple-element.32.kv_ref) | copy-start | bytes 1572868

commit v5 on v4

--- a/solution.py
+++ b/solution.py
@@ -150,11 +150,14 @@
 
 
 def main_kernel(
-    list_ref, slots_ref, query_t_ref, flag_ref, start_ref, query_s_ref, d_att_t_ref, out_t_ref,
+    list_in_ref, slots_ref, query_t_ref, flag_ref, start_ref, query_s_ref, d_att_t_ref, out_t_ref,
     grad_hbm, att_t_hbm, stat_hbm, kv_hbm,
-    grad_ref, att_t_ref, stat_ref, kv_ref, score_ref, weight_ref, d_score_ref, d_low_ref, sems,
+    list_ref, grad_ref, att_t_ref, stat_ref, kv_ref, score_ref, weight_ref, d_score_ref, d_low_ref, sems,
 ):
+    load = pltpu.make_async_copy(list_in_ref, list_ref, sems.at[5])
+    load.start()
     grad_ref[...] = jnp.zeros_like(grad_ref)
+    load.wait()
     for k in range(KEPT):
         kv_ref[k * TILE : (k + 1) * TILE, :] = slots_ref[list_ref[k]]
     value_t = kv_ref[:, HD:].T
@@ -173,9 +176,10 @@
 
     def weigh(n):
         total = jnp.zeros((TILE, PART), f32)
-        for rows in chunks:
+        for c in range(NEAR // 32):
+            rows = slice(c * 32, (c + 1) * 32)
             weights = jnp.exp2((score_ref[rows, parts[n]] - tops[n]) * SCALE)
-            total = total + jnp.sum(weights.reshape(CHUNK // TILE, TILE, PART), axis=0)
+            total = total + jnp.sum(weights.reshape(32 // TILE, TILE, PART), axis=0)
             weight_ref[rows, parts[n]] = weights.astype(bf16)
         totals.append(jnp.sum(total, axis=0, keepdims=True))
         outs.append(dot(value_t, weight_ref[:, parts[n]]))
@@ -209,7 +213,6 @@
         if n > 0:
             back(n - 1)
         finish(n)
-    back(N_PART - 1)
     stores = [
         pltpu.make_async_copy(att_t_ref, att_t_hbm, sems.at[1]),
         pltpu.make_async_copy(stat_ref, stat_hbm, sems.at[2]),
@@ -233,6 +236,7 @@
     for c in range(N_CHUNK):
         scatter(dot(weight_ref[chunks[c], :], d_low_ref[...]).astype(bf16), c, 1)
     send(1)
+    back(N_PART - 1)
     for c in range(N_CHUNK):
         scatter((dot(d_score_ref[chunks[c], :], query_s_ref[...]) * FACTOR).astype(bf16), c, 0)
     send(0)
@@ -327,12 +331,13 @@
     )
     grads, att_t, stat, near = call(
         main_kernel,
-        [(SMEM, places), (VMEM, fetched), (VMEM, query_t), (VMEM, flags), (VMEM, start), (VMEM, query_s), (VMEM, d_att_t),
+        [(VMEM, places), (VMEM, fetched), (VMEM, query_t), (VMEM, flags), (VMEM, start), (VMEM, query_s), (VMEM, d_att_t),
          (VMEM, out_t)],
         [(HBM, (SLOTS, TILE, 2 * HD), bf16), (HBM, (HD, WIDE), bf16), (HBM, (8, WIDE), f32), (HBM, (NEAR, 2 * HD), bf16)],
-        [VMEM((SLOTS, TILE, 2 * HD), bf16), VMEM((HD, WIDE), bf16), VMEM((8, WIDE), f32), VMEM((NEAR, 2 * HD), bf16),
+        [SMEM((KEPT,), jnp.int32), VMEM((SLOTS, TILE, 2 * HD), bf16), VMEM((HD, WIDE), bf16), VMEM((8, WIDE), f32),
+         VMEM((NEAR, 2 * HD), bf16),
          VMEM((NEAR, WIDE), f32), VMEM((NEAR, WIDE), bf16), VMEM((NEAR, WIDE), bf16), VMEM((WIDE, HD), bf16),
-         pltpu.SemaphoreType.DMA((5,))],
+         pltpu.SemaphoreType.DMA((6,))],
         2**30, 2**22, limit=VMEM_LIMIT,
     )
     returned = exchange(grads.reshape(PEERS, SECTIONS, TILE, 2 * HD)).reshape(KEYS, 2 * HD)

time: 90.9 us -> 90.7 us (level)
  no operation moved by 1% of the time
where the time goes in v5:
time: 90.7 us; the launch traced here: 90.3 us
  waiting for transfers between devices  37.9 us (42%)
  starting transfers between devices  23.4 us (26%)
  Pallas kernels  18.5 us (20%)
  blocking collectives  7.38 us (8%)
  local copies, waits for them, and re-layouts  1.73 us (2%)
    all_to_all x2, waiting for transfers between devices, exchange(): lax.all_to_all(pieces, 'ctx', split_axis=0, concat_axis=0, tiled=True)  37.9 us
    all_to_all x2, starting transfers between devices, exchange(): lax.all_to_all(pieces, 'ctx', split_axis=0, concat_axis=0, tiled=True)  23.4 us
    pallas_call x5, Pallas kernels, call(): pl.pallas_call(kernel, out_shape=[HBM(shape, kind) if space is HBM else j...  18.5 us
    all_gather x1, blocking collectives, body(): gate_sum = lax.all_gather(gate_part[0], 'head').sum(0)  7.38 us
  transfers between devices with their start and end apart: 2, of which 2 were waited for; matrix products, arithmetic and copies ran while one was open for 1% of the time, Pallas kernels for 12%

profile of v5, /device:TPU:6, one launch (start us, length us, event | category | flops | bytes accessed | tf_op | source)
XLA Modules:
  0.0 90.3 jit_solution(17521838794514426456)
XLA Ops:
  0.6 2.4 %send_kernel.1 = bf16[2048,256]{1,0:T(8,128)(2,1)} custom-call(s32[64,4,64]{2,1,0:T(4,128)} %plan_ref.1, bf16[128,128]{1,0:T(8,128)(2,1)} %key_ref.3, bf16[128,128]{1,0:T(8,128)(2,1)} %value_ref.3), custom_call_target="tpu_custom_call" | custom-call | flops 134217728 | bytes 2097152 | tf_op jit(solution)/shard_map/send_kernel/pallas_call | solution.py:293
  3.0 0.0 copy-start
  3.0 0.0 copy-start.1
  3.0 0.0 copy-start.2
  3.0 0.0 copy-start.3
  3.0 0.0 copy-start.4
  3.1 16.7 %all-to-all-start = ((bf16[64,4,8,256]{3,2,1,0:T(8,128)(2,1)}), bf16[64,4,8,256]{3,2,1,0:T(8,128)(2,1)S(1)}, u32[]{:S(2)}, u32[]{:S(2)}) async-start(bf16[64,4,8,256]{3,2,1,0:T(8,128)(2,1)} %bitcast.14), calls=%async_computation | async-start | bytes 2097152 | tf_op jit(solution)/shard_map/all_to_all | solution.py:307
  19.8 0.0 copy-done
  19.8 0.0 copy-start.5
  19.8 0.0 copy-start.6
  19.9 0.0 copy-done.1
  19.9 0.0 copy-done.2
  19.9 0.0 copy-done.3
  19.9 0.0 copy-done.4
  19.9 0.6 copy-done.5
  20.5 0.0 copy-done.6
  20.5 8.1 %local_kernel.1 = (bf16[256,768]{1,0:T(8,128)(2,1)S(1)}, bf16[768,128]{1,0:T(8,128)(2,1)S(1)}, bf16[128,768]{1,0:T(8,128)(2,1)S(1)}, bf16[1024,128]{1,0:T(8,128)...) custom-call(s32[4,64]{1,0:T(4,128)S(1)} %dynamic-slice_bitcast_fusio, ...), custom_call_target="tpu_custom_call" | custom-call | flops 134217728 | bytes 4194304 | tf_op jit(solution)/shard_map/local_kernel/pallas_call | solution.py:293
  28.7 20.9 %all-to-all-done = bf16[64,4,8,256]{3,2,1,0:T(8,128)(2,1)S(1)} async-done(((bf16[64,4,8,256]{3,2,1,0:T(8,128)(2,1)}), bf16[64,4,8,256]{3,2,1,0:T(8,128)(2,1)S(1)}, u32[]{:S(2)}, u32[]{:S(2)}) %all-to-all-start) | async-done | bytes 1048608 | tf_op jit(solution)/shard_map/all_to_all | solution.py:307
  49.6 4.2 %main_kernel.1 = (bf16[256,8,256]{2,1,0:T(8,128)(2,1)}, bf16[128,768]{1,0:T(8,128)(2,1)}, f32[8,768]{1,0:T(8,128)}, bf16[1024,256]{1,0:T(8,128)(2,1)}) custom-call(s32[128]{0:T(128)S(1)} %get-tuple-element.25.list_in_ref, bf16[256,8,256]{2,1,0:T(8,128)(2,1)S(1)} %bitcast.10, bf16[256,768]{1,0:T(8,128)(2,1)S(1)} %get-tuple-element.26.query_t_ref, ...), custom_call_target="tpu_custom_call" | custom-call | flops 1073741824 | bytes 4194304 | tf_op jit(solution)/shard_map/main_kernel/pallas_call | solution.py:293
  53.8 0.0 copy-start.7
  53.8 0.0 copy-start.8
  53.8 0.0 copy-start.9
  53.8 0.0 copy-start.10
  53.8 0.0 copy-start.12
  53.8 0.0 copy-start.13
  53.8 6.6 %all-to-all-start.1 = ((bf16[64,4,8,256]{3,2,1,0:T(8,128)(2,1)}), bf16[64,4,8,256]{3,2,1,0:T(8,128)(2,1)S(1)}, u32[]{:S(2)}, u32[]{:S(2)}) async-start(bf16[64,4,8,256]{3,2,1,0:T(8,128)(2,1)} %bitcast.15), calls=%async_computation.1 | async-start | bytes 2097152 | tf_op jit(solution)/shard_map/all_to_all | solution.py:307
  60.5 0.0 copy-done.7
  60.5 0.0 copy-done.8
  60.5 0.0 copy-done.9
  60.5 0.0 copy-done.10
  60.5 0.0 copy-done.12
  60.5 0.0 copy-done.13
  60.5 0.0 copy-start.11
  60.6 1.0 %copy-done.11 = bf16[1024,256]{1,0:T(8,128)(2,1)S(1)} copy-done((bf16[1024,256]{1,0:T(8,128)(2,1)S(1)}, bf16[1024,256]{1,0:T(8,128)(2,1)}, u32[]{:S(2)}) %copy-start.11) | copy-done | bytes 524312
  61.6 2.8 %query_kernel.1 = (bf16[128,768]{1,0:T(8,128)(2,1)}, f32[128,256]{1,0:T(8,128)S(1)}, f32[1,128]{1,0:T(1,128)S(1)}, bf16[128,2048]{1,0:T(8,128)(2,1)S(1)}) custom-call(s32[64,4,64]{2,1,0:T(4,128)S(1)} %copy-done, bf16[1024,256]{1,0:T(8,128)(2,1)S(1)} %copy-done.11, bf16[128,128]{1,0:T(8,128)(2,1)S(1)} %copy-done.1, bf16[128,128]{1,0:T(8,128)(2,1)S(1)} %copy-done.2, ...), custom_call_target="tpu_custom_call" | custom-call | flops 1073741824 | bytes 4194304 | tf_op jit(solution)/shard_map/query_kernel/pallas_call | solution.py:293
  64.4 7.4 %all-gather = f32[8,1,128]{2,1,0:T(1,128)S(1)} all-gather(f32[1,1,128]{2,1,0:T(1,128)S(1)} %bitcast.11), channel_id=1, replica_groups=mesh['head'=8,'ctx'=64] {'head'}, dimensions={0}, use_global_device_ids=true | all-gather | bytes 4608 | tf_op jit(solution)/shard_map/all_gather | solution.py:353
  71.8 0.5 fusion
  72.3 17.0 %all-to-all-done.1 = bf16[64,4,8,256]{3,2,1,0:T(8,128)(2,1)S(1)} async-done(((bf16[64,4,8,256]{3,2,1,0:T(8,128)(2,1)}), bf16[64,4,8,256]{3,2,1,0:T(8,128)(2,1)S(1)}, u32[]{:S(2)}, u32[]{:S(2)}) %all-to-all-start.1) | async-done | bytes 1048608 | tf_op jit(solution)/shard_map/all_to_all | solution.py:307
  89.4 0.9 %owner_kernel.1 = (bf16[128,128]{1,0:T(8,128)(2,1)}, bf16[128,128]{1,0:T(8,128)(2,1)}) custom-call(bf16[128,2048]{1,0:T(8,128)(2,1)S(1)} %get-tuple-element.40.owner_ref, bf16[2048,256]{1,0:T(8,128)(2,1)S(1)} %bitcast.9, f32[128,256]{1,0:T(8,128)S(1)} %get-tuple-element.42.local_ref), custom_call_target="tpu_custom_call" | custom-call | flops 134217728 | bytes 2097152 | tf_op jit(solution)/shard_map/owner_kernel/pallas_call | solution.py:293
  (2 shorter events, 0.0 us)
Async XLA Ops:
  3.0 16.8 %copy-start = (s32[64,4,64]{2,1,0:T(4,128)S(1)}, s32[64,4,64]{2,1,0:T(4,128)}, u32[]{:S(2)}) copy-start(s32[64,4,64]{2,1,0:T(4,128)} %plan_ref.1) | copy-start | bytes 196612
  3.0 16.8 %copy-start.1 = (bf16[128,128]{1,0:T(8,128)(2,1)S(1)}, bf16[128,128]{1,0:T(8,128)(2,1)}, u32[]{:S(2)}) copy-start(bf16[128,128]{1,0:T(8,128)(2,1)} %key_ref.3) | copy-start | bytes 98308
  3.0 16.8 %copy-start.2 = (bf16[128,128]{1,0:T(8,128)(2,1)S(1)}, bf16[128,128]{1,0:T(8,128)(2,1)}, u32[]{:S(2)}) copy-start(bf16[128,128]{1,0:T(8,128)(2,1)} %value_ref.3) | copy-start | bytes 98308
  3.0 16.8 %copy-start.3 = (bf16[128,768]{1,0:T(8,128)(2,1)S(1)}, bf16[128,768]{1,0:T(8,128)(2,1)}, u32[]{:S(2)}) copy-start(bf16[128,768]{1,0:T(8,128)(2,1)} %query_ref.1) | copy-start | bytes 589828
  3.0 16.8 %copy-start.4 = (bf16[128,768]{1,0:T(8,128)(2,1)S(1)}, bf16[128,768]{1,0:T(8,128)(2,1)}, u32[]{:S(2)}) copy-start(bf16[128,768]{1,0:T(8,128)(2,1)} %grad_ref.3) | copy-start | bytes 589828
  3.1 46.5 %all-to-all-start = ((bf16[64,4,8,256]{3,2,1,0:T(8,128)(2,1)}), bf16[64,4,8,256]{3,2,1,0:T(8,128)(2,1)S(1)}, u32[]{:S(2)}, u32[]{:S(2)}) async-start(bf16[64,4,8,256]{3,2,1,0:T(8,128)(2,1)} %bitcast.14), calls=%async_computation | async-start | bytes 2097152 | tf_op jit(solution)/shard_map/all_to_all | solution.py:307
  19.8 0.7 copy-start.5
  19.8 0.7 copy-start.6
  53.8 6.7 %copy-start.7 = (bf16[256,768]{1,0:T(8,128)(2,1)S(1)}, bf16[256,768]{1,0:T(8,128)(2,1)}, u32[]{:S(2)}) copy-start(bf16[256,768]{1,0:T(8,128)(2,1)} %get-tuple-element.33.query_t_ref) | copy-start | bytes 1179652
  53.8 6.7 %copy-start.8 = (bf16[1024,128]{1,0:T(8,128)(2,1)S(1)}, bf16[1024,128]{1,0:T(8,128)(2,1)}, u32[]{:S(2)}) copy-start(bf16[1024,128]{1,0:T(8,128)(2,1)} %get-tuple-element.36.flag_ref) | copy-start | bytes 786436
  53.8 6.7 %copy-start.9 = (bf16[768,128]{1,0:T(8,128)(2,1)S(1)}, bf16[768,128]{1,0:T(8,128)(2,1)}, u32[]{:S(2)}) copy-start(bf16[768,128]{1,0:T(8,128)(2,1)} %get-tuple-element.34.query_s_ref) | copy-start | bytes 589828
  53.8 6.7 %copy-start.10 = (bf16[128,768]{1,0:T(8,128)(2,1)S(1)}, bf16[128,768]{1,0:T(8,128)(2,1)}, u32[]{:S(2)}) copy-start(bf16[128,768]{1,0:T(8,128)(2,1)} %get-tuple-element.35.d_att_t_ref) | copy-start | bytes 589828
  53.8 6.7 %copy-start.12 = (bf16[128,768]{1,0:T(8,128)(2,1)S(1)}, bf16[128,768]{1,0:T(8,128)(2,1)}, u32[]{:S(2)}) copy-start(bf16[128,768]{1,0:T(8,128)(2,1)} %get-tuple-element.37.att_t_ref) | copy-start | bytes 589828
  53.8 6.7 %copy-start.13 = (f32[8,768]{1,0:T(8,128)S(1)}, f32[8,768]{1,0:T(8,128)}, u32[]{:S(2)}) copy-start(f32[8,768]{1,0:T(8,128)} %get-tuple-element.38.stat_ref) | copy-start | bytes 73732
  53.8 35.5 %all-to-all-start.1 = ((bf16[64,4,8,256]{3,2,1,0:T(8,128)(2,1)}), bf16[64,4,8,256]{3,2,1,0:T(8,128)(2,1)S(1)}, u32[]{:S(2)}, u32[]{:S(2)}) async-start(bf16[64,4,8,256]{3,2,1,0:T(8,128)(2,1)} %bitcast.15), calls=%async_computation.1 | async-start | bytes 2097152 | tf_op jit(solution)/shard_map/all_to_all | solution.py:307
  60.5 1.0 %copy-start.11 = (bf16[1024,256]{1,0:T(8,128)(2,1)S(1)}, bf16[1024,256]{1,0:T(8,128)(2,1)}, u32[]{:S(2)}) copy-start(bf16[1024,256]{1,0:T(8,128)(2,1)} %get-tuple-element.32.kv_ref) | copy-start | bytes 1572868

commit v6 on v5

--- a/solution.py
+++ b/solution.py
@@ -19,7 +19,7 @@
 KEPT = SECTIONS * PICKS
 NEAR = KEPT * TILE
 WIDE = GROUP * ROWS
-CHUNK = 256
+CHUNK = PICKS * TILE
 PART = 256
 N_CHUNK = NEAR // CHUNK
 N_PART = WIDE // PART
@@ -122,14 +122,14 @@
 
         @pl.loop(0, PICKS)
         def _(k):
-            list_ref[s * PICKS + k] = device * SECTIONS + s
+            list_ref[s * PICKS + k] = device
 
         def place(p, count):
             given = plan_ref[s, p] >= 0
 
             @pl.when(given)
             def _():
-                list_ref[s * PICKS + count] = p * SECTIONS + s
+                list_ref[s * PICKS + count] = p
                 at = pl.multiple_of((s * PICKS + count) * TILE, TILE)
                 chosen = jnp.where(kind_ref[s, p] == 0, -1, 1)
                 flag_ref[pl.ds(at, TILE), :] = (lane == chosen).astype(bf16)
@@ -154,12 +154,12 @@
     grad_hbm, att_t_hbm, stat_hbm, kv_hbm,
     list_ref, grad_ref, att_t_ref, stat_ref, kv_ref, score_ref, weight_ref, d_score_ref, d_low_ref, sems,
 ):
-    load = pltpu.make_async_copy(list_in_ref, list_ref, sems.at[5])
+    load = pltpu.make_async_copy(list_in_ref, list_ref, sems.at[3])
     load.start()
     grad_ref[...] = jnp.zeros_like(grad_ref)
     load.wait()
     for k in range(KEPT):
-        kv_ref[k * TILE : (k + 1) * TILE, :] = slots_ref[list_ref[k]]
+        kv_ref[k * TILE : (k + 1) * TILE, :] = slots_ref[list_ref[k], k // PICKS]
     value_t = kv_ref[:, HD:].T
     chunks = [slice(c * CHUNK, (c + 1) * CHUNK) for c in range(N_CHUNK)]
     parts = [slice(n * PART, (n + 1) * PART) for n in range(N_PART)]
@@ -214,32 +214,25 @@
             back(n - 1)
         finish(n)
     stores = [
+        pltpu.make_async_copy(kv_ref, kv_hbm, sems.at[0]),
         pltpu.make_async_copy(att_t_ref, att_t_hbm, sems.at[1]),
         pltpu.make_async_copy(stat_ref, stat_hbm, sems.at[2]),
-        pltpu.make_async_copy(kv_ref, kv_hbm, sems.at[0]),
     ]
-
-    def scatter(values, c, side):
-        for k in range(CHUNK // TILE):
-            slot = list_ref[c * (CHUNK // TILE) + k]
-            grad_ref[slot, :, side * HD : (side + 1) * HD] = values[k * TILE : (k + 1) * TILE, :]
-
-    def send(side):
-        half = pl.ds(side * HD, HD)
-        stores.append(
-            pltpu.make_async_copy(grad_ref.at[:, :, half], grad_hbm.at[:, :, half], sems.at[3 + side])
-        )
+    for store in stores:
+        store.start()
+
+    def scatter(values, s, side):
+        for k in range(PICKS):
+            block = list_ref[s * PICKS + k]
+            grad_ref[block, s, :, side * HD : (side + 1) * HD] = values[k * TILE : (k + 1) * TILE, :]
+
+    for s in range(SECTIONS):
+        scatter(dot(weight_ref[chunks[s], :], d_low_ref[...]).astype(bf16), s, 1)
+    back(N_PART - 1)
+    for s in range(SECTIONS):
+        scatter((dot(d_score_ref[chunks[s], :], query_s_ref[...]) * FACTOR).astype(bf16), s, 0)
+        stores.append(pltpu.make_async_copy(grad_ref.at[:, s], grad_hbm.at[:, s], sems.at[4 + s]))
         stores[-1].start()
-
-    for store in stores:
-        store.start()
-    for c in range(N_CHUNK):
-        scatter(dot(weight_ref[chunks[c], :], d_low_ref[...]).astype(bf16), c, 1)
-    send(1)
-    back(N_PART - 1)
-    for c in range(N_CHUNK):
-        scatter((dot(d_score_ref[chunks[c], :], query_s_ref[...]) * FACTOR).astype(bf16), c, 0)
-    send(0)
     for store in stores:
         store.wait()
 
@@ -319,7 +312,7 @@
          VMEM((SLOTS, PEERS), f32), pltpu.SemaphoreType.DMA((3 + SEND_PARTS,))],
         2**27, 2**21,
     )
-    fetched = exchange(outgoing.reshape(PEERS, SECTIONS, TILE, 2 * HD)).reshape(SLOTS, TILE, 2 * HD)
+    fetched = exchange(outgoing.reshape(PEERS, SECTIONS, TILE, 2 * HD))
     query_t, query_s, d_att_t, flags, start, out_t, places, *again = call(
         local_kernel,
         [(SMEM, plan_row), (SMEM, mask_kind[0]), (VMEM, queries), (VMEM, key_rows), (VMEM, value_rows),
@@ -333,14 +326,15 @@
         main_kernel,
         [(VMEM, places), (VMEM, fetched), (VMEM, query_t), (VMEM, flags), (VMEM, start), (VMEM, query_s), (VMEM, d_att_t),
          (VMEM, out_t)],
-        [(HBM, (SLOTS, TILE, 2 * HD), bf16), (HBM, (HD, WIDE), bf16), (HBM, (8, WIDE), f32), (HBM, (NEAR, 2 * HD), bf16)],
-        [SMEM((KEPT,), jnp.int32), VMEM((SLOTS, TILE, 2 * HD), bf16), VMEM((HD, WIDE), bf16), VMEM((8, WIDE), f32),
+        [(HBM, (PEERS, SECTIONS, TILE, 2 * HD), bf16), (HBM, (HD, WIDE), bf16), (HBM, (8, WIDE), f32),
+         (HBM, (NEAR, 2 * HD), bf16)],
+        [SMEM((KEPT,), jnp.int32), VMEM((PEERS, SECTIONS, TILE, 2 * HD), bf16), VMEM((HD, WIDE), bf16), VMEM((8, WIDE), f32),
          VMEM((NEAR, 2 * HD), bf16),
          VMEM((NEAR, WIDE), f32), VMEM((NEAR, WIDE), bf16), VMEM((NEAR, WIDE), bf16), VMEM((WIDE, HD), bf16),
-         pltpu.SemaphoreType.DMA((6,))],
+         pltpu.SemaphoreType.DMA((8,))],
         2**30, 2**22, limit=VMEM_LIMIT,
     )
-    returned = exchange(grads.reshape(PEERS, SECTIONS, TILE, 2 * HD)).reshape(KEYS, 2 * HD)
+    returned = exchange(grads).reshape(KEYS, 2 * HD)
     query_grad, local, gate_part, owner = call(
         query_kernel,
         [(VMEM, tile_plan), (VMEM, near), (VMEM, key_rows), (VMEM, value_rows), (VMEM, out_grad),

time: 90.7 us -> 90.6 us (level)
  no operation moved by 1% of the time
where the time goes in v6:
time: 90.6 us; the launch traced here: 90.2 us
  waiting for transfers between devices  38 us (42%)
  starting transfers between devices  23.4 us (26%)
  Pallas kernels  18.3 us (20%)
  blocking collectives  7.38 us (8%)
  local copies, waits for them, and re-layouts  1.73 us (2%)
    all_to_all x2, waiting for transfers between devices, exchange(): lax.all_to_all(pieces, 'ctx', split_axis=0, concat_axis=0, tiled=True)  38 us
    all_to_all x2, starting transfers between devices, exchange(): lax.all_to_all(pieces, 'ctx', split_axis=0, concat_axis=0, tiled=True)  23.4 us
    pallas_call x5, Pallas kernels, call(): pl.pallas_call(kernel, out_shape=[HBM(shape, kind) if space is HBM else j...  18.3 us
    all_gather x1, blocking collectives, body(): gate_sum = lax.all_gather(gate_part[0], 'head').sum(0)  7.38 us
  transfers between devices with their start and end apart: 2, of which 2 were waited for; matrix products, arithmetic and copies ran while one was open for 1% of the time, Pallas kernels for 12%

profile of v6, /device:TPU:6, one launch (start us, length us, event | category | flops | bytes accessed | tf_op | source)
XLA Modules:
  0.0 90.2 jit_solution(8188485782192285641)
XLA Ops:
  0.6 2.4 %send_kernel.1 = bf16[2048,256]{1,0:T(8,128)(2,1)} custom-call(s32[64,4,64]{2,1,0:T(4,128)} %plan_ref.1, bf16[128,128]{1,0:T(8,128)(2,1)} %key_ref.3, bf16[128,128]{1,0:T(8,128)(2,1)} %value_ref.3), custom_call_target="tpu_custom_call" | custom-call | flops 134217728 | bytes 2097152 | tf_op jit(solution)/shard_map/send_kernel/pallas_call | solution.py:286
  3.0 0.0 copy-start
  3.0 0.0 copy-start.1
  3.0 0.0 copy-start.2
  3.0 0.0 copy-start.3
  3.0 0.0 copy-start.4
  3.1 16.7 %all-to-all-start = ((bf16[64,4,8,256]{3,2,1,0:T(8,128)(2,1)}), bf16[64,4,8,256]{3,2,1,0:T(8,128)(2,1)S(1)}, u32[]{:S(2)}, u32[]{:S(2)}) async-start(bf16[64,4,8,256]{3,2,1,0:T(8,128)(2,1)} %bitcast.11), calls=%async_computation | async-start | bytes 2097152 | tf_op jit(solution)/shard_map/all_to_all | solution.py:300
  19.8 0.0 copy-done
  19.8 0.0 copy-start.5
  19.8 0.0 copy-start.6
  19.9 0.0 copy-done.1
  19.9 0.0 copy-done.2
  19.9 0.0 copy-done.3
  19.9 0.0 copy-done.4
  19.9 0.6 copy-done.5
  20.5 0.0 copy-done.6
  20.5 8.0 %local_kernel.1 = (bf16[256,768]{1,0:T(8,128)(2,1)S(1)}, bf16[768,128]{1,0:T(8,128)(2,1)S(1)}, bf16[128,768]{1,0:T(8,128)(2,1)S(1)}, bf16[1024,128]{1,0:T(8,128)...) custom-call(s32[4,64]{1,0:T(4,128)S(1)} %dynamic-slice_bitcast_fusio, ...), custom_call_target="tpu_custom_call" | custom-call | flops 134217728 | bytes 4194304 | tf_op jit(solution)/shard_map/local_kernel/pallas_call | solution.py:286
  28.6 21.0 %all-to-all-done.slots_ref = bf16[64,4,8,256]{3,2,1,0:T(8,128)(2,1)S(1)} async-done(((bf16[64,4,8,256]{3,2,1,0:T(8,128)(2,1)}), bf16[64,4,8,256]{3,2,1,0:T(8,128)(2,1)S(1)}, u32[]{:S(2)}, u32[]{:S(2)}) %all-to-all-start) | async-done | bytes 1048608 | tf_op jit(solution)/shard_map/all_to_all | solution.py:300
  49.6 4.1 %main_kernel.1 = (bf16[64,4,8,256]{3,2,1,0:T(8,128)(2,1)}, bf16[128,768]{1,0:T(8,128)(2,1)}, f32[8,768]{1,0:T(8,128)}, bf16[1024,256]{1,0:T(8,128)(2,1)}) custom-call(s32[128]{0:T(128)S(1)} %get-tuple-element.25.list_in_ref, bf16[64,4,8,256]{3,2,1,0:T(8,128)(2,1)S(1)} %all-to-all-done.slots_ref, bf16[256,768]{1,0:T(8,128)(2,1)S(1)} %get-tuple-element.26.query_t_ref, ...), custom_call_target="tpu_custom_call" | custom-call | flops 1073741824 | bytes 4194304 | tf_op jit(solution)/shard_map/main_kernel/pallas_call | solution.py:286
  53.7 0.0 copy-start.7
  53.7 0.0 copy-start.8
  53.7 0.0 copy-start.9
  53.7 0.0 copy-start.10
  53.8 0.0 copy-start.12
  53.8 0.0 copy-start.13
  53.8 6.6 %all-to-all-start.1 = ((bf16[64,4,8,256]{3,2,1,0:T(8,128)(2,1)}), bf16[64,4,8,256]{3,2,1,0:T(8,128)(2,1)S(1)}, u32[]{:S(2)}, u32[]{:S(2)}) async-start(bf16[64,4,8,256]{3,2,1,0:T(8,128)(2,1)} %get-tuple-element.41), calls=%async_computation.1 | async-start | bytes 2097152 | tf_op jit(solution)/shard_map/all_to_all | solution.py:300
  60.4 0.0 copy-done.7
  60.4 0.0 copy-done.8
  60.4 0.0 copy-done.9
  60.4 0.0 copy-done.10
  60.5 0.0 copy-done.12
  60.5 0.0 copy-done.13
  60.5 0.0 copy-start.11
  60.5 1.0 %copy-done.11 = bf16[1024,256]{1,0:T(8,128)(2,1)S(1)} copy-done((bf16[1024,256]{1,0:T(8,128)(2,1)S(1)}, bf16[1024,256]{1,0:T(8,128)(2,1)}, u32[]{:S(2)}) %copy-start.11) | copy-done | bytes 524312
  61.5 2.8 %query_kernel.1 = (bf16[128,768]{1,0:T(8,128)(2,1)}, f32[128,256]{1,0:T(8,128)S(1)}, f32[1,128]{1,0:T(1,128)S(1)}, bf16[128,2048]{1,0:T(8,128)(2,1)S(1)}) custom-call(s32[64,4,64]{2,1,0:T(4,128)S(1)} %copy-done, bf16[1024,256]{1,0:T(8,128)(2,1)S(1)} %copy-done.11, bf16[128,128]{1,0:T(8,128)(2,1)S(1)} %copy-done.1, bf16[128,128]{1,0:T(8,128)(2,1)S(1)} %copy-done.2, ...), custom_call_target="tpu_custom_call" | custom-call | flops 1073741824 | bytes 4194304 | tf_op jit(solution)/shard_map/query_kernel/pallas_call | solution.py:286
  64.3 7.4 %all-gather = f32[8,1,128]{2,1,0:T(1,128)S(1)} all-gather(f32[1,1,128]{2,1,0:T(1,128)S(1)} %bitcast.8), channel_id=1, replica_groups=mesh['head'=8,'ctx'=64] {'head'}, dimensions={0}, use_global_device_ids=true | all-gather | bytes 4608 | tf_op jit(solution)/shard_map/all_gather | solution.py:347
  71.7 0.5 fusion
  72.3 17.0 %all-to-all-done.1 = bf16[64,4,8,256]{3,2,1,0:T(8,128)(2,1)S(1)} async-done(((bf16[64,4,8,256]{3,2,1,0:T(8,128)(2,1)}), bf16[64,4,8,256]{3,2,1,0:T(8,128)(2,1)S(1)}, u32[]{:S(2)}, u32[]{:S(2)}) %all-to-all-start.1) | async-done | bytes 1048608 | tf_op jit(solution)/shard_map/all_to_all | solution.py:300
  89.3 0.9 %owner_kernel.1 = (bf16[128,128]{1,0:T(8,128)(2,1)}, bf16[128,128]{1,0:T(8,128)(2,1)}) custom-call(bf16[128,2048]{1,0:T(8,128)(2,1)S(1)} %get-tuple-element.40.owner_ref, bf16[2048,256]{1,0:T(8,128)(2,1)S(1)} %bitcast.7, f32[128,256]{1,0:T(8,128)S(1)} %get-tuple-element.42.local_ref), custom_call_target="tpu_custom_call" | custom-call | flops 134217728 | bytes 2097152 | tf_op jit(solution)/shard_map/owner_kernel/pallas_call | solution.py:286
  (2 shorter events, 0.0 us)
Async XLA Ops:
  3.0 16.8 %copy-start = (s32[64,4,64]{2,1,0:T(4,128)S(1)}, s32[64,4,64]{2,1,0:T(4,128)}, u32[]{:S(2)}) copy-start(s32[64,4,64]{2,1,0:T(4,128)} %plan_ref.1) | copy-start | bytes 196612
  3.0 16.8 %copy-start.1 = (bf16[128,128]{1,0:T(8,128)(2,1)S(1)}, bf16[128,128]{1,0:T(8,128)(2,1)}, u32[]{:S(2)}) copy-start(bf16[128,128]{1,0:T(8,128)(2,1)} %key_ref.3) | copy-start | bytes 98308
  3.0 16.8 %copy-start.2 = (bf16[128,128]{1,0:T(8,128)(2,1)S(1)}, bf16[128,128]{1,0:T(8,128)(2,1)}, u32[]{:S(2)}) copy-start(bf16[128,128]{1,0:T(8,128)(2,1)} %value_ref.3) | copy-start | bytes 98308
  3.0 16.8 %copy-start.3 = (bf16[128,768]{1,0:T(8,128)(2,1)S(1)}, bf16[128,768]{1,0:T(8,128)(2,1)}, u32[]{:S(2)}) copy-start(bf16[128,768]{1,0:T(8,128)(2,1)} %query_ref.1) | copy-start | bytes 589828
  3.0 16.8 %copy-start.4 = (bf16[128,768]{1,0:T(8,128)(2,1)S(1)}, bf16[128,768]{1,0:T(8,128)(2,1)}, u32[]{:S(2)}) copy-start(bf16[128,768]{1,0:T(8,128)(2,1)} %grad_ref.3) | copy-start | bytes 589828
  3.1 46.5 %all-to-all-start = ((bf16[64,4,8,256]{3,2,1,0:T(8,128)(2,1)}), bf16[64,4,8,256]{3,2,1,0:T(8,128)(2,1)S(1)}, u32[]{:S(2)}, u32[]{:S(2)}) async-start(bf16[64,4,8,256]{3,2,1,0:T(8,128)(2,1)} %bitcast.11), calls=%async_computation | async-start | bytes 2097152 | tf_op jit(solution)/shard_map/all_to_all | solution.py:300
  19.8 0.7 copy-start.5
  19.8 0.7 copy-start.6
  53.7 6.7 %copy-start.7 = (bf16[256,768]{1,0:T(8,128)(2,1)S(1)}, bf16[256,768]{1,0:T(8,128)(2,1)}, u32[]{:S(2)}) copy-start(bf16[256,768]{1,0:T(8,128)(2,1)} %get-tuple-element.33.query_t_ref) | copy-start | bytes 1179652
  53.7 6.7 %copy-start.8 = (bf16[1024,128]{1,0:T(8,128)(2,1)S(1)}, bf16[1024,128]{1,0:T(8,128)(2,1)}, u32[]{:S(2)}) copy-start(bf16[1024,128]{1,0:T(8,128)(2,1)} %get-tuple-element.36.flag_ref) | copy-start | bytes 786436
  53.7 6.7 %copy-start.9 = (bf16[768,128]{1,0:T(8,128)(2,1)S(1)}, bf16[768,128]{1,0:T(8,128)(2,1)}, u32[]{:S(2)}) copy-start(bf16[768,128]{1,0:T(8,128)(2,1)} %get-tuple-element.34.query_s_ref) | copy-start | bytes 589828
  53.7 6.7 %copy-start.10 = (bf16[128,768]{1,0:T(8,128)(2,1)S(1)}, bf16[128,768]{1,0:T(8,128)(2,1)}, u32[]{:S(2)}) copy-start(bf16[128,768]{1,0:T(8,128)(2,1)} %get-tuple-element.35.d_att_t_ref) | copy-start | bytes 589828
  53.8 6.7 %copy-start.12 = (bf16[128,768]{1,0:T(8,128)(2,1)S(1)}, bf16[128,768]{1,0:T(8,128)(2,1)}, u32[]{:S(2)}) copy-start(bf16[128,768]{1,0:T(8,128)(2,1)} %get-tuple-element.37.att_t_ref) | copy-start | bytes 589828
  53.8 6.7 %copy-start.13 = (f32[8,768]{1,0:T(8,128)S(1)}, f32[8,768]{1,0:T(8,128)}, u32[]{:S(2)}) copy-start(f32[8,768]{1,0:T(8,128)} %get-tuple-element.38.stat_ref) | copy-start | bytes 73732
  53.8 35.5 %all-to-all-start.1 = ((bf16[64,4,8,256]{3,2,1,0:T(8,128)(2,1)}), bf16[64,4,8,256]{3,2,1,0:T(8,128)(2,1)S(1)}, u32[]{:S(2)}, u32[]{:S(2)}) async-start(bf16[64,4,8,256]{3,2,1,0:T(8,128)(2,1)} %get-tuple-element.41), calls=%async_computation.1 | async-start | bytes 2097152 | tf_op jit(solution)/shard_map/all_to_all | solution.py:300
  60.5 1.0 %copy-start.11 = (bf16[1024,256]{1,0:T(8,128)(2,1)S(1)}, bf16[1024,256]{1,0:T(8,128)(2,1)}, u32[]{:S(2)}) copy-start(bf16[1024,256]{1,0:T(8,128)(2,1)} %get-tuple-element.32.kv_ref) | copy-start | bytes 1572868

commit v7 on v6

--- a/solution.py
+++ b/solution.py
@@ -210,9 +210,9 @@
         if n + 1 < N_PART:
             score(n + 1)
         weigh(n)
+        finish(n)
         if n > 0:
             back(n - 1)
-        finish(n)
     stores = [
         pltpu.make_async_copy(kv_ref, kv_hbm, sems.at[0]),
         pltpu.make_async_copy(att_t_ref, att_t_hbm, sems.at[1]),
@@ -226,9 +226,9 @@
             block = list_ref[s * PICKS + k]
             grad_ref[block, s, :, side * HD : (side + 1) * HD] = values[k * TILE : (k + 1) * TILE, :]
 
+    back(N_PART - 1)
     for s in range(SECTIONS):
         scatter(dot(weight_ref[chunks[s], :], d_low_ref[...]).astype(bf16), s, 1)
-    back(N_PART - 1)
     for s in range(SECTIONS):
         scatter((dot(d_score_ref[chunks[s], :], query_s_ref[...]) * FACTOR).astype(bf16), s, 0)
         stores.append(pltpu.make_async_copy(grad_ref.at[:, s], grad_hbm.at[:, s], sems.at[4 + s]))

time: 90.6 us -> 90.5 us (level)
  no operation moved by 1% of the time
where the time goes in v7:
time: 90.5 us; the launch traced here: 90.1 us
  waiting for transfers between devices  38 us (42%)
  starting transfers between devices  23.4 us (26%)
  Pallas kernels  18.2 us (20%)
  blocking collectives  7.38 us (8%)
  local copies, waits for them, and re-layouts  1.73 us (2%)
    all_to_all x2, waiting for transfers between devices, exchange(): lax.all_to_all(pieces, 'ctx', split_axis=0, concat_axis=0, tiled=True)  38 us
    all_to_all x2, starting transfers between devices, exchange(): lax.all_to_all(pieces, 'ctx', split_axis=0, concat_axis=0, tiled=True)  23.4 us
    pallas_call x5, Pallas kernels, call(): pl.pallas_call(kernel, out_shape=[HBM(shape, kind) if space is HBM else j...  18.2 us
    all_gather x1, blocking collectives, body(): gate_sum = lax.all_gather(gate_part[0], 'head').sum(0)  7.38 us
  transfers between devices with their start and end apart: 2, of which 2 were waited for; matrix products, arithmetic and copies ran while one was open for 1% of the time, Pallas kernels for 12%

profile of v7, /device:TPU:6, one launch (start us, length us, event | category | flops | bytes accessed | tf_op | source)
XLA Modules:
  0.0 90.1 jit_solution(4390432782312539368)
XLA Ops:
  0.6 2.4 %send_kernel.1 = bf16[2048,256]{1,0:T(8,128)(2,1)} custom-call(s32[64,4,64]{2,1,0:T(4,128)} %plan_ref.1, bf16[128,128]{1,0:T(8,128)(2,1)} %key_ref.3, bf16[128,128]{1,0:T(8,128)(2,1)} %value_ref.3), custom_call_target="tpu_custom_call" | custom-call | flops 134217728 | bytes 2097152 | tf_op jit(solution)/shard_map/send_kernel/pallas_call | solution.py:286
  3.0 0.0 copy-start
  3.0 0.0 copy-start.1
  3.0 0.0 copy-start.2
  3.0 0.0 copy-start.3
  3.0 0.0 copy-start.4
  3.1 16.7 %all-to-all-start = ((bf16[64,4,8,256]{3,2,1,0:T(8,128)(2,1)}), bf16[64,4,8,256]{3,2,1,0:T(8,128)(2,1)S(1)}, u32[]{:S(2)}, u32[]{:S(2)}) async-start(bf16[64,4,8,256]{3,2,1,0:T(8,128)(2,1)} %bitcast.11), calls=%async_computation | async-start | bytes 2097152 | tf_op jit(solution)/shard_map/all_to_all | solution.py:300
  19.8 0.0 copy-done
  19.8 0.0 copy-start.5
  19.8 0.0 copy-start.6
  19.9 0.0 copy-done.1
  19.9 0.0 copy-done.2
  19.9 0.0 copy-done.3
  19.9 0.0 copy-done.4
  19.9 0.6 copy-done.5
  20.5 0.0 copy-done.6
  20.5 8.1 %local_kernel.1 = (bf16[256,768]{1,0:T(8,128)(2,1)S(1)}, bf16[768,128]{1,0:T(8,128)(2,1)S(1)}, bf16[128,768]{1,0:T(8,128)(2,1)S(1)}, bf16[1024,128]{1,0:T(8,128)...) custom-call(s32[4,64]{1,0:T(4,128)S(1)} %dynamic-slice_bitcast_fusio, ...), custom_call_target="tpu_custom_call" | custom-call | flops 134217728 | bytes 4194304 | tf_op jit(solution)/shard_map/local_kernel/pallas_call | solution.py:286
  28.6 20.9 %all-to-all-done.slots_ref = bf16[64,4,8,256]{3,2,1,0:T(8,128)(2,1)S(1)} async-done(((bf16[64,4,8,256]{3,2,1,0:T(8,128)(2,1)}), bf16[64,4,8,256]{3,2,1,0:T(8,128)(2,1)S(1)}, u32[]{:S(2)}, u32[]{:S(2)}) %all-to-all-start) | async-done | bytes 1048608 | tf_op jit(solution)/shard_map/all_to_all | solution.py:300
  49.6 4.0 %main_kernel.1 = (bf16[64,4,8,256]{3,2,1,0:T(8,128)(2,1)}, bf16[128,768]{1,0:T(8,128)(2,1)}, f32[8,768]{1,0:T(8,128)}, bf16[1024,256]{1,0:T(8,128)(2,1)}) custom-call(s32[128]{0:T(128)S(1)} %get-tuple-element.25.list_in_ref, bf16[64,4,8,256]{3,2,1,0:T(8,128)(2,1)S(1)} %all-to-all-done.slots_ref, bf16[256,768]{1,0:T(8,128)(2,1)S(1)} %get-tuple-element.26.query_t_ref, ...), custom_call_target="tpu_custom_call" | custom-call | flops 1073741824 | bytes 4194304 | tf_op jit(solution)/shard_map/main_kernel/pallas_call | solution.py:286
  53.6 0.0 copy-start.7
  53.6 0.0 copy-start.8
  53.6 0.0 copy-start.9
  53.6 0.0 copy-start.10
  53.6 0.0 copy-start.12
  53.6 0.0 copy-start.13
  53.7 6.6 %all-to-all-start.1 = ((bf16[64,4,8,256]{3,2,1,0:T(8,128)(2,1)}), bf16[64,4,8,256]{3,2,1,0:T(8,128)(2,1)S(1)}, u32[]{:S(2)}, u32[]{:S(2)}) async-start(bf16[64,4,8,256]{3,2,1,0:T(8,128)(2,1)} %get-tuple-element.41), calls=%async_computation.1 | async-start | bytes 2097152 | tf_op jit(solution)/shard_map/all_to_all | solution.py:300
  60.3 0.0 copy-done.7
  60.3 0.0 copy-done.8
  60.3 0.0 copy-done.9
  60.3 0.0 copy-done.10
  60.3 0.0 copy-done.12
  60.4 0.0 copy-done.13
  60.4 0.0 copy-start.11
  60.4 1.0 %copy-done.11 = bf16[1024,256]{1,0:T(8,128)(2,1)S(1)} copy-done((bf16[1024,256]{1,0:T(8,128)(2,1)S(1)}, bf16[1024,256]{1,0:T(8,128)(2,1)}, u32[]{:S(2)}) %copy-start.11) | copy-done | bytes 524312
  61.4 2.8 %query_kernel.1 = (bf16[128,768]{1,0:T(8,128)(2,1)}, f32[128,256]{1,0:T(8,128)S(1)}, f32[1,128]{1,0:T(1,128)S(1)}, bf16[128,2048]{1,0:T(8,128)(2,1)S(1)}) custom-call(s32[64,4,64]{2,1,0:T(4,128)S(1)} %copy-done, bf16[1024,256]{1,0:T(8,128)(2,1)S(1)} %copy-done.11, bf16[128,128]{1,0:T(8,128)(2,1)S(1)} %copy-done.1, bf16[128,128]{1,0:T(8,128)(2,1)S(1)} %copy-done.2, ...), custom_call_target="tpu_custom_call" | custom-call | flops 1073741824 | bytes 4194304 | tf_op jit(solution)/shard_map/query_kernel/pallas_call | solution.py:286
  64.2 7.4 %all-gather = f32[8,1,128]{2,1,0:T(1,128)S(1)} all-gather(f32[1,1,128]{2,1,0:T(1,128)S(1)} %bitcast.8), channel_id=1, replica_groups=mesh['head'=8,'ctx'=64] {'head'}, dimensions={0}, use_global_device_ids=true | all-gather | bytes 4608 | tf_op jit(solution)/shard_map/all_gather | solution.py:347
  71.6 0.5 fusion
  72.2 17.0 %all-to-all-done.1 = bf16[64,4,8,256]{3,2,1,0:T(8,128)(2,1)S(1)} async-done(((bf16[64,4,8,256]{3,2,1,0:T(8,128)(2,1)}), bf16[64,4,8,256]{3,2,1,0:T(8,128)(2,1)S(1)}, u32[]{:S(2)}, u32[]{:S(2)}) %all-to-all-start.1) | async-done | bytes 1048608 | tf_op jit(solution)/shard_map/all_to_all | solution.py:300
  89.2 0.9 %owner_kernel.1 = (bf16[128,128]{1,0:T(8,128)(2,1)}, bf16[128,128]{1,0:T(8,128)(2,1)}) custom-call(bf16[128,2048]{1,0:T(8,128)(2,1)S(1)} %get-tuple-element.40.owner_ref, bf16[2048,256]{1,0:T(8,128)(2,1)S(1)} %bitcast.7, f32[128,256]{1,0:T(8,128)S(1)} %get-tuple-element.42.local_ref), custom_call_target="tpu_custom_call" | custom-call | flops 134217728 | bytes 2097152 | tf_op jit(solution)/shard_map/owner_kernel/pallas_call | solution.py:286
  (2 shorter events, 0.0 us)
Async XLA Ops:
  3.0 16.8 %copy-start = (s32[64,4,64]{2,1,0:T(4,128)S(1)}, s32[64,4,64]{2,1,0:T(4,128)}, u32[]{:S(2)}) copy-start(s32[64,4,64]{2,1,0:T(4,128)} %plan_ref.1) | copy-start | bytes 196612
  3.0 16.8 %copy-start.1 = (bf16[128,128]{1,0:T(8,128)(2,1)S(1)}, bf16[128,128]{1,0:T(8,128)(2,1)}, u32[]{:S(2)}) copy-start(bf16[128,128]{1,0:T(8,128)(2,1)} %key_ref.3) | copy-start | bytes 98308
  3.0 16.8 %copy-start.2 = (bf16[128,128]{1,0:T(8,128)(2,1)S(1)}, bf16[128,128]{1,0:T(8,128)(2,1)}, u32[]{:S(2)}) copy-start(bf16[128,128]{1,0:T(8,128)(2,1)} %value_ref.3) | copy-start | bytes 98308
  3.0 16.8 %copy-start.3 = (bf16[128,768]{1,0:T(8,128)(2,1)S(1)}, bf16[128,768]{1,0:T(8,128)(2,1)}, u32[]{:S(2)}) copy-start(bf16[128,768]{1,0:T(8,128)(2,1)} %query_ref.1) | copy-start | bytes 589828
  3.0 16.8 %copy-start.4 = (bf16[128,768]{1,0:T(8,128)(2,1)S(1)}, bf16[128,768]{1,0:T(8,128)(2,1)}, u32[]{:S(2)}) copy-start(bf16[128,768]{1,0:T(8,128)(2,1)} %grad_ref.3) | copy-start | bytes 589828
  3.1 46.5 %all-to-all-start = ((bf16[64,4,8,256]{3,2,1,0:T(8,128)(2,1)}), bf16[64,4,8,256]{3,2,1,0:T(8,128)(2,1)S(1)}, u32[]{:S(2)}, u32[]{:S(2)}) async-start(bf16[64,4,8,256]{3,2,1,0:T(8,128)(2,1)} %bitcast.11), calls=%async_computation | async-start | bytes 2097152 | tf_op jit(solution)/shard_map/all_to_all | solution.py:300
  19.8 0.7 copy-start.5
  19.8 0.7 copy-start.6
  53.6 6.7 %copy-start.7 = (bf16[256,768]{1,0:T(8,128)(2,1)S(1)}, bf16[256,768]{1,0:T(8,128)(2,1)}, u32[]{:S(2)}) copy-start(bf16[256,768]{1,0:T(8,128)(2,1)} %get-tuple-element.33.query_t_ref) | copy-start | bytes 1179652
  53.6 6.7 %copy-start.8 = (bf16[1024,128]{1,0:T(8,128)(2,1)S(1)}, bf16[1024,128]{1,0:T(8,128)(2,1)}, u32[]{:S(2)}) copy-start(bf16[1024,128]{1,0:T(8,128)(2,1)} %get-tuple-element.36.flag_ref) | copy-start | bytes 786436
  53.6 6.7 %copy-start.9 = (bf16[768,128]{1,0:T(8,128)(2,1)S(1)}, bf16[768,128]{1,0:T(8,128)(2,1)}, u32[]{:S(2)}) copy-start(bf16[768,128]{1,0:T(8,128)(2,1)} %get-tuple-element.34.query_s_ref) | copy-start | bytes 589828
  53.6 6.7 %copy-start.10 = (bf16[128,768]{1,0:T(8,128)(2,1)S(1)}, bf16[128,768]{1,0:T(8,128)(2,1)}, u32[]{:S(2)}) copy-start(bf16[128,768]{1,0:T(8,128)(2,1)} %get-tuple-element.35.d_att_t_ref) | copy-start | bytes 589828
  53.6 6.7 %copy-start.12 = (bf16[128,768]{1,0:T(8,128)(2,1)S(1)}, bf16[128,768]{1,0:T(8,128)(2,1)}, u32[]{:S(2)}) copy-start(bf16[128,768]{1,0:T(8,128)(2,1)} %get-tuple-element.37.att_t_ref) | copy-start | bytes 589828
  53.6 6.7 %copy-start.13 = (f32[8,768]{1,0:T(8,128)S(1)}, f32[8,768]{1,0:T(8,128)}, u32[]{:S(2)}) copy-start(f32[8,768]{1,0:T(8,128)} %get-tuple-element.38.stat_ref) | copy-start | bytes 73732
  53.7 35.5 %all-to-all-start.1 = ((bf16[64,4,8,256]{3,2,1,0:T(8,128)(2,1)}), bf16[64,4,8,256]{3,2,1,0:T(8,128)(2,1)S(1)}, u32[]{:S(2)}, u32[]{:S(2)}) async-start(bf16[64,4,8,256]{3,2,1,0:T(8,128)(2,1)} %get-tuple-element.41), calls=%async_computation.1 | async-start | bytes 2097152 | tf_op jit(solution)/shard_map/all_to_all | solution.py:300
  60.4 1.0 %copy-start.11 = (bf16[1024,256]{1,0:T(8,128)(2,1)S(1)}, bf16[1024,256]{1,0:T(8,128)(2,1)}, u32[]{:S(2)}) copy-start(bf16[1024,256]{1,0:T(8,128)(2,1)} %get-tuple-element.32.kv_ref) | copy-start | bytes 1572868
